TPU v7x, 128 devices: a whole 4x4x4 slice. The times are simulated.
128 devices in a mesh: shard: 32 (over z, x, core), tensor: 4 (over y).
Axes of the slice: x: 4, y: 4, z: 4, core: 2. Of those that a mesh axis runs over, the one named last changes fastest.
Arguments:
- attn_grads: float32 [4, 2048, 2048], P(None, 'tensor', 'shard'), may hold values from -400 to 400
- mlp_grads: float32 [3, 5120, 2048], P(None, 'tensor', 'shard'), may hold values from -400 to 400
- attn_master: float32 [4, 4194304], P(None, ('shard', 'tensor')), may hold values from -0.75 to 0.75
- attn_first: float32 [4, 4194304], P(None, ('shard', 'tensor')), may hold values from -4 to 4
- attn_second: float32 [4, 4194304], P(None, ('shard', 'tensor')), may hold values from 0.01 to 1
- attn_average: float32 [4, 4194304], P(None, ('shard', 'tensor')), may hold values from -0.75 to 0.75
- mlp_master: float32 [3, 10485760], P(None, ('shard', 'tensor')), may hold values from -0.75 to 0.75
- mlp_first: float32 [3, 10485760], P(None, ('shard', 'tensor')), may hold values from -4 to 4
- mlp_second: float32 [3, 10485760], P(None, ('shard', 'tensor')), may hold values from 0.01 to 1
- mlp_average: float32 [3, 10485760], P(None, ('shard', 'tensor')), may hold values from -0.75 to 0.75
Outputs:
- attn_master_new: float32 [4, 4194304], P(None, ('shard', 'tensor'))
- attn_first_new: float32 [4, 4194304], P(None, ('shard', 'tensor'))
- attn_second_new: float32 [4, 4194304], P(None, ('shard', 'tensor'))
- attn_average_new: float32 [4, 4194304], P(None, ('shard', 'tensor'))
- mlp_master_new: float32 [3, 10485760], P(None, ('shard', 'tensor'))
- mlp_first_new: float32 [3, 10485760], P(None, ('shard', 'tensor'))
- mlp_second_new: float32 [3, 10485760], P(None, ('shard', 'tensor'))
- mlp_average_new: float32 [3, 10485760], P(None, ('shard', 'tensor'))
- attn_weights: bfloat16 [4, 2048, 2048], P(None, 'tensor', 'shard')
- mlp_weights: bfloat16 [3, 5120, 2048], P(None, 'tensor', 'shard')
All inputs are finite; a program needn't handle non-finite values.
Results may differ from a plain program's by a relative error of at most 0.0035.
Values may be sent and summed in bfloat16 or wider, within the bound.
A program may use at most 128 MiB of HBM per device.

v0:
```python
import jax
import jax.numpy as jnp
from jax import lax
from jax.sharding import PartitionSpec as P

D = 2048
STEP = 100
COUNT = 48234496


beta_one = 0.9
beta_two = 0.999
adam_eps = 1e-08
learn_rate = 0.01
decay_weight = 0.1
average_keep = 0.999
clip_level = 1.0


def advance(flat_grads, master, first_moment, second, average, clip_factor):
    clipped = clip_factor * flat_grads
    first_new = beta_one * first_moment + (1.0 - beta_one) * clipped
    second_new = beta_two * second + (1.0 - beta_two) * clipped * clipped
    update = (
        first_new
        / (1.0 - beta_one**STEP)
        / (jnp.sqrt(second_new / (1.0 - beta_two**STEP)) + adam_eps)
    )
    master_new = master - learn_rate * (update + decay_weight * master)
    average_new = average_keep * average + (1.0 - average_keep) * master_new
    return (master_new, first_new, second_new, average_new)


def total_squares(first_part, second_part):
    return lax.psum(
        (jnp.sum(first_part * first_part), jnp.sum(second_part * second_part)), ("shard", "tensor")
    )


def per_device(
    attn_grads,
    mlp_grads,
    attn_master,
    attn_first,
    attn_second,
    attn_average,
    mlp_master,
    mlp_first,
    mlp_second,
    mlp_average,
):
    shards = lax.axis_size("shard")
    tensors = lax.axis_size("tensor")
    across = shards // tensors

    def split_rows(grad_block):
        member_count, row_count, col_count = grad_block.shape
        piece_rows = row_count // shards
        return grad_block.reshape(member_count, 1, across, tensors, piece_rows, col_count)

    sectioned_attn, sectioned_mlp = (
        lax.all_to_all(
            split_rows(attn_grads).astype(jnp.bfloat16),
            "tensor",
            split_axis=3,
            concat_axis=1,
            tiled=True,
        ).astype(jnp.float32),
        lax.all_to_all(
            split_rows(mlp_grads).astype(jnp.bfloat16),
            "tensor",
            split_axis=3,
            concat_axis=1,
            tiled=True,
        ).astype(jnp.float32),
    )

    def by_shard(sectioned):
        return sectioned.reshape(sectioned.shape[0], shards, sectioned.shape[4], sectioned.shape[5])

    landed_attn, landed_mlp = (
        lax.all_to_all(
            by_shard(sectioned_attn).astype(jnp.bfloat16),
            "shard",
            split_axis=1,
            concat_axis=3,
            tiled=True,
        ).astype(jnp.float32),
        lax.all_to_all(
            by_shard(sectioned_mlp).astype(jnp.bfloat16),
            "shard",
            split_axis=1,
            concat_axis=3,
            tiled=True,
        ).astype(jnp.float32),
    )
    piece_attn = landed_attn.reshape(landed_attn.shape[0], -1)
    piece_mlp = landed_mlp.reshape(landed_mlp.shape[0], -1)
    square_sums = total_squares(piece_attn, piece_mlp)
    grand_total = square_sums[0] + square_sums[1]
    clip_factor = jnp.minimum(1.0, clip_level / jnp.sqrt(grand_total / COUNT + 1e-06))
    attn_out = advance(piece_attn, attn_master, attn_first, attn_second, attn_average, clip_factor)
    mlp_out = advance(piece_mlp, mlp_master, mlp_first, mlp_second, mlp_average, clip_factor)

    def to_return(master_new):
        member_count = master_new.shape[0]
        piece_rows = master_new.shape[1] // D
        return master_new.astype(jnp.bfloat16).reshape(member_count, 1, piece_rows, D)

    spread_attn, spread_mlp = (
        lax.all_to_all(to_return(attn_out[0]), "shard", split_axis=3, concat_axis=1, tiled=True),
        lax.all_to_all(to_return(mlp_out[0]), "shard", split_axis=3, concat_axis=1, tiled=True),
    )

    def by_tensor(spread):
        return spread.reshape(spread.shape[0], tensors, across, 1, spread.shape[2], spread.shape[3])

    back_attn, back_mlp = (
        lax.all_to_all(by_tensor(spread_attn), "tensor", split_axis=1, concat_axis=3, tiled=True),
        lax.all_to_all(by_tensor(spread_mlp), "tensor", split_axis=1, concat_axis=3, tiled=True),
    )
    attn_weights = back_attn.reshape(attn_grads.shape)
    mlp_weights = back_mlp.reshape(mlp_grads.shape)
    return (
        attn_out[0],
        attn_out[1],
        attn_out[2],
        attn_out[3],
        mlp_out[0],
        mlp_out[1],
        mlp_out[2],
        mlp_out[3],
        attn_weights,
        mlp_weights,
    )


def solution(mesh):
    placed = (
        P(None, "tensor", "shard"),
        P(None, "tensor", "shard"),
        P(None, ("shard", "tensor")),
        P(None, ("shard", "tensor")),
        P(None, ("shard", "tensor")),
        P(None, ("shard", "tensor")),
        P(None, ("shard", "tensor")),
        P(None, ("shard", "tensor")),
        P(None, ("shard", "tensor")),
        P(None, ("shard", "tensor")),
    )
    return jax.shard_map(
        per_device,
        mesh=mesh,
        in_specs=placed,
        out_specs=(
            P(None, ("shard", "tensor")),
            P(None, ("shard", "tensor")),
            P(None, ("shard", "tensor")),
            P(None, ("shard", "tensor")),
            P(None, ("shard", "tensor")),
            P(None, ("shard", "tensor")),
            P(None, ("shard", "tensor")),
            P(None, ("shard", "tensor")),
            P(None, "tensor", "shard"),
            P(None, "tensor", "shard"),
        ),
        check_vma=False,
    )
```

profile of v0, /device:TPU:1, one launch (start us, length us, event | category | flops | bytes accessed | tf_op | source)
XLA Modules:
  0.0 199.9 jit_solution(443528229080846164)
XLA Ops:
  0.6 1.3 copy.50
  2.0 0.0 copy-start.3
  2.0 1.1 reshape.112
  3.1 5.0 %all-to-all-start = ((bf16[4,2,16384]{2,1,0:T(2,128)(2,1)}), bf16[4,2,16384]{2,1,0:T(2,128)(2,1)S(1)}, u32[]{:S(2)}, u32[]{:S(2)}) async-start(bf16[4,2,16384]{2,1,0:T(2,128)(2,1)} %reshape.112), calls=%async_computation | async-start | bytes 524288 | tf_op jit(solution)/shard_map/all_to_all | solution.py:62
  8.2 0.5 copy.54
  8.6 0.1 copy.90
  8.8 1.5 reshape.116
  10.2 3.5 %all-to-all-done = bf16[4,2,16384]{2,1,0:T(2,128)(2,1)S(1)} async-done(((bf16[4,2,16384]{2,1,0:T(2,128)(2,1)}), bf16[4,2,16384]{2,1,0:T(2,128)(2,1)S(1)}, u32[]{:S(2)}, u32[]{:S(2)}) %all-to-all-start) | async-done | bytes 262176 | tf_op jit(solution)/shard_map/all_to_all | solution.py:62
  13.7 3.5 %all-to-all-start.2 = ((bf16[4,2,30720]{2,1,0:T(2,128)(2,1)}), bf16[4,2,30720]{2,1,0:T(2,128)(2,1)S(1)}, u32[]{:S(2)}, u32[]{:S(2)}) async-start(bf16[4,2,30720]{2,1,0:T(2,128)(2,1)} %reshape.116), calls=%async_computation.2 | async-start | bytes 983040 | tf_op jit(solution)/shard_map/all_to_all | solution.py:69
  17.2 0.3 reshape.113
  17.6 0.1 copy.92
  17.6 1.1 reshape.114
  18.8 5.2 %all-to-all-done.2 = bf16[4,2,30720]{2,1,0:T(2,128)(2,1)S(1)} async-done(((bf16[4,2,30720]{2,1,0:T(2,128)(2,1)}), bf16[4,2,30720]{2,1,0:T(2,128)(2,1)S(1)}, u32[]{:S(2)}, u32[]{:S(2)}) %all-to-all-start.2) | async-done | bytes 491552 | tf_op jit(solution)/shard_map/all_to_all | solution.py:69
  23.9 11.2 %all-to-all-start.1 = ((bf16[32,2,2048]{2,1,0:T(2,128)(2,1)}), bf16[32,2,2048]{2,1,0:T(2,128)(2,1)S(1)}, u32[]{:S(2)}, u32[]{:S(2)}) async-start(bf16[32,2,2048]{2,1,0:T(2,128)(2,1)} %reshape.114), calls=%async_computation.1 | async-start | bytes 524288 | tf_op jit(solution)/shard_map/all_to_all | solution.py:82
  35.2 0.6 reshape.117
  35.8 0.1 copy.56
  35.9 0.1 copy.89
  36.0 1.4 reshape.118
  37.3 6.7 %all-to-all-done.1 = bf16[32,2,2048]{2,1,0:T(2,128)(2,1)S(1)} async-done(((bf16[32,2,2048]{2,1,0:T(2,128)(2,1)}), bf16[32,2,2048]{2,1,0:T(2,128)(2,1)S(1)}, u32[]{:S(2)}, u32[]{:S(2)}) %all-to-all-start.1) | async-done | bytes 262176 | tf_op jit(solution)/shard_map/all_to_all | solution.py:82
  44.1 3.8 %all-to-all-start.3 = ((bf16[32,2,3840]{2,1,0:T(2,128)(2,1)}), bf16[32,2,3840]{2,1,0:T(2,128)(2,1)S(1)}, u32[]{:S(2)}, u32[]{:S(2)}) async-start(bf16[32,2,3840]{2,1,0:T(2,128)(2,1)} %reshape.118), calls=%async_computation.3 | async-start | bytes 983040 | tf_op jit(solution)/shard_map/all_to_all | solution.py:89
  47.8 0.4 reshape.115
  48.2 0.9 fusion.3
  49.1 10.1 %all-to-all-done.3 = bf16[32,2,3840]{2,1,0:T(2,128)(2,1)S(1)} async-done(((bf16[32,2,3840]{2,1,0:T(2,128)(2,1)}), bf16[32,2,3840]{2,1,0:T(2,128)(2,1)S(1)}, u32[]{:S(2)}, u32[]{:S(2)}) %all-to-all-start.3) | async-done | bytes 491552 | tf_op jit(solution)/shard_map/all_to_all | solution.py:89
  59.2 0.6 reshape.119
  59.8 1.1 fusion
  62.2 63.1 %psum.16 = f32[]{:T(128)} all-reduce(f32[]{:T(128)S(6)} %add.46), channel_id=1, replica_groups=mesh['shard'=32,'tensor'=4] {'shard','tensor'}, use_global_device_ids=true, to_apply=%region_1.0 | all-reduce | flops 1 | bytes 8 | tf_op jit(solution)/shard_map/psum | solution.py:35
  126.0 0.1 fusion.4
  126.1 0.1 fusion.1
  126.2 0.6 copy.58
  126.8 1.2 mul.116
  128.1 1.6 copy.59
  129.7 2.6 %mul.132 = f32[3,81920]{1,0:T(4,128)S(1)} reshape(f32[3,1,40,32,64]{4,3,2,0,1:T(8,128)} %copy.59) | data formatting | bytes 1966080 | tf_op jit(solution)/shard_map/mul | solution.py:21
  132.4 1.9 fusion.8
  134.3 0.9 copy.87
  135.1 2.7 %copy.60 = bf16[4,1,16,2048]{2,0,1,3:T(4,128)(2,1)S(1)} copy(bf16[4,1,16,2048]{3,2,0,1:T(8,128)(2,1)} %bitcast.116) | data formatting | bytes 524288 | tf_op jit(solution)/shard_map/reshape | solution.py:108
  137.8 2.9 %reshape.120 = bf16[32,2,2048]{2,1,0:T(2,128)(2,1)} reshape(bf16[2048,1,4,16]{3,2,1,0:T(4,128)(2,1)S(1)} %bitcast.97) | data formatting | bytes 524288
  140.7 4.7 %all-to-all-start.4 = ((bf16[32,2,2048]{2,1,0:T(2,128)(2,1)}), bf16[32,2,2048]{2,1,0:T(2,128)(2,1)S(1)}, u32[]{:S(2)}, u32[]{:S(2)}) async-start(bf16[32,2,2048]{2,1,0:T(2,128)(2,1)} %reshape.120), calls=%async_computation.4 | async-start | bytes 524288 | tf_op jit(solution)/shard_map/all_to_all | solution.py:111
  145.4 5.0 %fusion.6 = (bf16[3,81920]{1,0:T(4,128)(2,1)S(1)}, f32[3,81920]{1,0:T(4,128)}, f32[3,81920]{1,0:T(4,128)}, f32[3,81920]{1,0:T(4,128)}) fusion(f32[3,81920]{1,0:T(4,128)} %param.16, f32[3,81920]{1,0:T(4,128)S(1)} %mul.132, f32[3,81920]{1,0:T(4,128)} %param.17, f32[3,81920]{1,0:T(4,128)} %param.18), kind=kLoop, calls=%fused_computation.20 | loop fusion | flops 3932160 | bytes 7372800 | tf_op jit(solution)/shard_map/convert_element_type | solution.py:108
  150.4 0.4 copy.86
  150.8 1.4 copy.65
  152.2 3.2 %reshape.124 = bf16[32,2,3840]{2,1,0:T(2,128)(2,1)} reshape(bf16[2048,1,3,40]{3,2,1,0:T(4,128)(2,1)S(1)} %bitcast.94) | data formatting | bytes 983040
  155.4 7.4 %all-to-all-start.6 = ((bf16[32,2,3840]{2,1,0:T(2,128)(2,1)}), bf16[32,2,3840]{2,1,0:T(2,128)(2,1)S(1)}, u32[]{:S(2)}, u32[]{:S(2)}) async-start(bf16[32,2,3840]{2,1,0:T(2,128)(2,1)} %reshape.124), calls=%async_computation.6 | async-start | bytes 983040 | tf_op jit(solution)/shard_map/all_to_all | solution.py:112
  162.8 1.4 reshape.121
  164.2 1.3 copy.73
  165.5 0.0 copy-start
  165.6 1.1 reshape.122
  166.7 7.3 %all-to-all-done.6 = bf16[32,2,3840]{2,1,0:T(2,128)(2,1)S(1)} async-done(((bf16[32,2,3840]{2,1,0:T(2,128)(2,1)}), bf16[32,2,3840]{2,1,0:T(2,128)(2,1)S(1)}, u32[]{:S(2)}, u32[]{:S(2)}) %all-to-all-start.6) | async-done | bytes 491552 | tf_op jit(solution)/shard_map/all_to_all | solution.py:112
  174.0 3.6 %all-to-all-start.5 = ((bf16[4,2,16384]{2,1,0:T(2,128)(2,1)}), bf16[4,2,16384]{2,1,0:T(2,128)(2,1)S(1)}, u32[]{:S(2)}, u32[]{:S(2)}) async-start(bf16[4,2,16384]{2,1,0:T(2,128)(2,1)} %reshape.122), calls=%async_computation.5 | async-start | bytes 524288 | tf_op jit(solution)/shard_map/all_to_all | solution.py:119
  177.6 2.9 %multiply_add_fusion = f32[3,81920]{1,0:T(4,128)} fusion(f32[3,81920]{1,0:T(4,128)S(1)} %copy-done, f32[3,81920]{1,0:T(4,128)} %param.19), kind=kLoop, calls=%fused_computation.8 | loop fusion | flops 737280 | bytes 2949120 | tf_op jit(solution)/shard_map/add | solution.py:30
  180.6 2.6 %reshape.125 = bf16[2048,1,3,40]{3,2,1,0:T(4,128)(2,1)S(1)} reshape(bf16[32,2,3840]{2,1,0:T(2,128)(2,1)S(1)} %all-to-all-done.6) | data formatting | bytes 983040
  183.2 1.3 copy.75
  184.5 0.1 copy.88
  184.6 0.0 copy-start.1
  184.6 1.5 reshape.126
  186.1 4.0 %all-to-all-start.7 = ((bf16[4,2,30720]{2,1,0:T(2,128)(2,1)}), bf16[4,2,30720]{2,1,0:T(2,128)(2,1)S(1)}, u32[]{:S(2)}, u32[]{:S(2)}) async-start(bf16[4,2,30720]{2,1,0:T(2,128)(2,1)} %reshape.126), calls=%async_computation.7 | async-start | bytes 983040 | tf_op jit(solution)/shard_map/all_to_all | solution.py:120
  190.0 1.0 multiply_add_fusion.2
  191.1 0.3 reshape.123
  191.5 0.1 copy.64
  191.5 0.9 copy.70
  192.4 5.5 %all-to-all-done.7 = bf16[4,2,30720]{2,1,0:T(2,128)(2,1)S(1)} async-done(((bf16[4,2,30720]{2,1,0:T(2,128)(2,1)}), bf16[4,2,30720]{2,1,0:T(2,128)(2,1)S(1)}, u32[]{:S(2)}, u32[]{:S(2)}) %all-to-all-start.7) | async-done | bytes 491552 | tf_op jit(solution)/shard_map/all_to_all | solution.py:120
  197.9 0.6 reshape.127
  198.5 0.1 bitcast_bitcast_fusion
  198.6 0.1 copy.69
  198.7 1.1 copy.71
  (19 shorter events, 0.2 us)
Async XLA Ops:
  2.0 6.2 %copy-start.3 = (f32[3,1280,64]{1,2,0:T(8,128)S(1)}, f32[3,1280,64]{1,2,0:T(8,128)}, u32[]{:S(2)}) copy-start(f32[3,1280,64]{1,2,0:T(8,128)} %param.11) | copy-start | bytes 2949124
  3.1 10.6 %all-to-all-start = ((bf16[4,2,16384]{2,1,0:T(2,128)(2,1)}), bf16[4,2,16384]{2,1,0:T(2,128)(2,1)S(1)}, u32[]{:S(2)}, u32[]{:S(2)}) async-start(bf16[4,2,16384]{2,1,0:T(2,128)(2,1)} %reshape.112), calls=%async_computation | async-start | bytes 524288 | tf_op jit(solution)/shard_map/all_to_all | solution.py:62
  13.7 10.2 %all-to-all-start.2 = ((bf16[4,2,30720]{2,1,0:T(2,128)(2,1)}), bf16[4,2,30720]{2,1,0:T(2,128)(2,1)S(1)}, u32[]{:S(2)}, u32[]{:S(2)}) async-start(bf16[4,2,30720]{2,1,0:T(2,128)(2,1)} %reshape.116), calls=%async_computation.2 | async-start | bytes 983040 | tf_op jit(solution)/shard_map/all_to_all | solution.py:69
  23.9 20.1 %all-to-all-start.1 = ((bf16[32,2,2048]{2,1,0:T(2,128)(2,1)}), bf16[32,2,2048]{2,1,0:T(2,128)(2,1)S(1)}, u32[]{:S(2)}, u32[]{:S(2)}) async-start(bf16[32,2,2048]{2,1,0:T(2,128)(2,1)} %reshape.114), calls=%async_computation.1 | async-start | bytes 524288 | tf_op jit(solution)/shard_map/all_to_all | solution.py:82
  44.1 15.1 %all-to-all-start.3 = ((bf16[32,2,3840]{2,1,0:T(2,128)(2,1)}), bf16[32,2,3840]{2,1,0:T(2,128)(2,1)S(1)}, u32[]{:S(2)}, u32[]{:S(2)}) async-start(bf16[32,2,3840]{2,1,0:T(2,128)(2,1)} %reshape.118), calls=%async_computation.3 | async-start | bytes 983040 | tf_op jit(solution)/shard_map/all_to_all | solution.py:89
  129.7 2.6 %copy-start.2 = (f32[4,32768]{1,0:T(4,128)S(1)}, f32[4,32768]{1,0:T(4,128)}, u32[]{:S(2)}) copy-start(f32[4,32768]{1,0:T(4,128)} %mul.116) | copy-start | bytes 1572868
  129.7 2.6 %copy-start.4 = (f32[4,32768]{1,0:T(4,128)S(1)}, f32[4,32768]{1,0:T(4,128)}, u32[]{:S(2)}) copy-start(f32[4,32768]{1,0:T(4,128)} %param.12) | copy-start | bytes 1572868
  129.7 2.6 %copy-start.5 = (f32[4,32768]{1,0:T(4,128)S(1)}, f32[4,32768]{1,0:T(4,128)}, u32[]{:S(2)}) copy-start(f32[4,32768]{1,0:T(4,128)} %param.13) | copy-start | bytes 1572868
  129.7 2.6 %copy-start.6 = (f32[4,32768]{1,0:T(4,128)S(1)}, f32[4,32768]{1,0:T(4,128)}, u32[]{:S(2)}) copy-start(f32[4,32768]{1,0:T(4,128)} %param.14) | copy-start | bytes 1572868
  140.7 14.7 %all-to-all-start.4 = ((bf16[32,2,2048]{2,1,0:T(2,128)(2,1)}), bf16[32,2,2048]{2,1,0:T(2,128)(2,1)S(1)}, u32[]{:S(2)}, u32[]{:S(2)}) async-start(bf16[32,2,2048]{2,1,0:T(2,128)(2,1)} %reshape.120), calls=%async_computation.4 | async-start | bytes 524288 | tf_op jit(solution)/shard_map/all_to_all | solution.py:111
  155.4 18.6 %all-to-all-start.6 = ((bf16[32,2,3840]{2,1,0:T(2,128)(2,1)}), bf16[32,2,3840]{2,1,0:T(2,128)(2,1)S(1)}, u32[]{:S(2)}, u32[]{:S(2)}) async-start(bf16[32,2,3840]{2,1,0:T(2,128)(2,1)} %reshape.124), calls=%async_computation.6 | async-start | bytes 983040 | tf_op jit(solution)/shard_map/all_to_all | solution.py:112
  165.5 12.1 %copy-start = (f32[3,81920]{1,0:T(4,128)S(1)}, f32[3,81920]{1,0:T(4,128)}, u32[]{:S(2)}) copy-start(f32[3,81920]{1,0:T(4,128)} %get-tuple-element.51) | copy-start | bytes 2949124
  174.0 12.1 %all-to-all-start.5 = ((bf16[4,2,16384]{2,1,0:T(2,128)(2,1)}), bf16[4,2,16384]{2,1,0:T(2,128)(2,1)S(1)}, u32[]{:S(2)}, u32[]{:S(2)}) async-start(bf16[4,2,16384]{2,1,0:T(2,128)(2,1)} %reshape.122), calls=%async_computation.5 | async-start | bytes 524288 | tf_op jit(solution)/shard_map/all_to_all | solution.py:119
  184.6 5.5 %copy-start.1 = (f32[4,32768]{1,0:T(4,128)S(1)}, f32[4,32768]{1,0:T(4,128)}, u32[]{:S(2)}) copy-start(f32[4,32768]{1,0:T(4,128)} %get-tuple-element.55) | copy-start | bytes 1572868
  184.6 5.5 %copy-start.7 = (f32[4,32768]{1,0:T(4,128)S(1)}, f32[4,32768]{1,0:T(4,128)}, u32[]{:S(2)}) copy-start(f32[4,32768]{1,0:T(4,128)} %param.15) | copy-start | bytes 1572868
  186.1 11.9 %all-to-all-start.7 = ((bf16[4,2,30720]{2,1,0:T(2,128)(2,1)}), bf16[4,2,30720]{2,1,0:T(2,128)(2,1)S(1)}, u32[]{:S(2)}, u32[]{:S(2)}) async-start(bf16[4,2,30720]{2,1,0:T(2,128)(2,1)} %reshape.126), calls=%async_computation.7 | async-start | bytes 983040 | tf_op jit(solution)/shard_map/all_to_all | solution.py:120
where the time goes:
time: 202 us; the launch traced here: 200 us
  blocking collectives  63.1 us (31%)
  starting transfers between devices  43.2 us (21%)
  local copies, waits for them, and re-layouts  39.2 us (19%)
  waiting for transfers between devices  38.3 us (19%)
  other arithmetic  13.1 us (6%)
  between operations  3 us (1%)
    psum x1, blocking collectives, total_squares(): lax.psum((jnp.sum(first_part * first_part), jnp.sum(second_part * second_...  63.1 us
    unnamed x38, local copies, waits for them, and re-layouts  25.6 us
    all_to_all x1, starting transfers between devices, per_device(): lax.all_to_all(by_shard(sectioned_attn).astype(jnp.bfloat16), 'shard', sp...  11.2 us
    all_to_all x1, waiting for transfers between devices, per_device(): lax.all_to_all(by_shard(sectioned_mlp).astype(jnp.bfloat16), 'shard', spl...  10.1 us
    all_to_all x1, starting transfers between devices, per_device(): lax.all_to_all(to_return(mlp_out[0]), 'shard', split_axis=3, concat_axis=...  7.38 us
    all_to_all x1, waiting for transfers between devices, per_device(): lax.all_to_all(to_return(mlp_out[0]), 'shard', split_axis=3, concat_axis=...  7.3 us
    convert_element_type x2, other arithmetic, to_return(): master_new.astype(jnp.bfloat16).reshape(member_count, 1, piece_rows, D)  6.92 us
    all_to_all x1, waiting for transfers between devices, per_device(): lax.all_to_all(by_shard(sectioned_attn).astype(jnp.bfloat16), 'shard', sp...  6.72 us
  transfers between devices with their start and end apart: 8, of which 6 were waited for; matrix products, arithmetic and copies ran while one was open for 16% of the time, Pallas kernels for 0%

commit v1 on v0

v1 whole, which is shorter than its diff:
```python
import functools

import jax
import jax.numpy as jnp
from jax import lax
from jax.experimental import pallas as pl
from jax.experimental.pallas import tpu as pltpu
from jax.sharding import PartitionSpec as P

D = 2048
STEP = 100
COUNT = 48234496

beta_one = 0.9
beta_two = 0.999
adam_eps = 1e-08
learn_rate = 0.01
decay_weight = 0.1
average_keep = 0.999
clip_level = 1.0

MESH = pl.DeviceIdType.MESH
ROWS = 96
F32 = jnp.float32
BF16 = jnp.bfloat16


def advance(grads, master, first, second, clip):
    clipped = clip * grads
    first_new = beta_one * first + (1.0 - beta_one) * clipped
    second_new = beta_two * second + (1.0 - beta_two) * clipped * clipped
    update = (first_new * (1.0 / (1.0 - beta_one**STEP))) / (
        jnp.sqrt(second_new * (1.0 / (1.0 - beta_two**STEP))) + adam_eps
    )
    master_new = master - learn_rate * (update + decay_weight * master)
    return master_new, first_new, second_new


def low_lanes(rows):
    return lax.broadcasted_iota(jnp.int32, (rows, 128), 1) < 64


def split_halves(p_zero, p_one):
    low = low_lanes(p_zero.shape[0])
    return jnp.where(low, p_zero, p_one), pltpu.roll(jnp.where(low, p_one, p_zero), 64, 1)


def position():
    s = lax.axis_index("shard")
    return s // 8, (s // 2) % 4, s % 2, lax.axis_index("tensor")


def device(z, x, c, y):
    return (z * 8 + x * 2 + c, y)


def wait_for(ref, sem):
    pltpu.make_async_copy(ref, ref, sem).wait()


OTHERS = [(dx, dc) for dx in range(4) for dc in range(2)][1:]


class Exchange:
    def __init__(self, forward, held, landed, a_recv, b_recv, c_recv, a_sent, b_sent, c_sent):
        self.held, self.landed = held, landed
        self.a_recv, self.b_recv, self.c_recv = a_recv, b_recv, c_recv
        self.a_sent, self.b_sent, self.c_sent = a_sent, b_sent, c_sent
        self.z, self.x, self.c, self.y = position()
        self.forward = forward
        self.a, self.b = (self.y, self.z) if forward else (self.z, self.y)
        self.mine = self.x * 2 + self.c

    def at(self, a, x, c, b):
        return device(b, x, c, a) if self.forward else device(a, x, c, b)

    def send_a(self, da, xc):
        pltpu.make_async_remote_copy(
            src_ref=self.held.at[3 + da, xc],
            dst_ref=self.held.at[da, xc],
            send_sem=self.a_sent,
            recv_sem=self.a_recv.at[da, xc],
            device_id=self.at((self.a + da) % 4, self.x, self.c, self.b),
            device_id_type=MESH,
        ).start()

    def pass_b(self, da):
        origin = (self.a + 4 - da) % 4
        slot = jnp.where(origin == self.b, origin, 4 + origin)

        def take(xc):
            if da:
                wait_for(self.held.at[da, xc], self.a_recv.at[da, xc])

        for dx, dc in OTHERS:
            x, c = (self.x + dx) % 4, (self.c + dc) % 2
            xc = x * 2 + c
            take(xc)
            pltpu.make_async_remote_copy(
                src_ref=self.held.at[da, xc],
                dst_ref=self.landed.at[slot, self.mine],
                send_sem=self.b_sent.at[da],
                recv_sem=self.b_recv.at[origin, self.mine],
                device_id=self.at(self.a, x, c, self.b),
                device_id_type=MESH,
            ).start()
        take(self.mine)
        pltpu.make_async_copy(
            self.held.at[da, self.mine],
            self.landed.at[slot, self.mine],
            self.b_recv.at[origin, self.mine],
        ).start()

    def pass_c(self, da):
        origin = (self.a + 4 - da) % 4
        slot = jnp.where(origin == self.b, origin, 4 + origin)
        for xc in range(8):
            wait_for(self.landed.at[slot, xc], self.b_recv.at[origin, xc])

            @pl.when(origin != self.b)
            def _():
                pltpu.make_async_remote_copy(
                    src_ref=self.landed.at[slot, xc],
                    dst_ref=self.landed.at[self.b, xc],
                    send_sem=self.c_sent,
                    recv_sem=self.c_recv.at[self.b, xc],
                    device_id=self.at(self.a, self.x, self.c, origin),
                    device_id_type=MESH,
                ).start()

    def take_c(self, source, xc):
        wait_for(self.landed.at[source, xc], self.c_recv.at[source, xc])

    def drain(self):
        wait_for(self.held.at[pl.ds(4, 3)], self.a_sent)
        for da in range(4):
            wait_for(self.held.at[da, pl.ds(0, 7)], self.b_sent.at[da])
        wait_for(self.held.at[pl.ds(4, 3)], self.c_sent)


def exchange_kernel(
    attn_grads,
    mlp_grads,
    attn_master,
    attn_first,
    attn_second,
    mlp_master,
    mlp_first,
    mlp_second,
    attn_out,
    mlp_out,
    clip_out,
    back,
    stack_attn,
    stack_mlp,
    turned_attn,
    turned_mlp,
    held,
    landed,
    held_back,
    state_attn,
    state_mlp,
    flat_attn,
    flat_mlp,
    sums,
    grad_sem,
    state_sem,
    flat_sem,
    sum_recv,
    sum_sent,
    fa_recv,
    fb_recv,
    fc_recv,
    fa_sent,
    fb_sent,
    fc_sent,
    ra_recv,
    rb_recv,
    rc_recv,
    ra_sent,
    rb_sent,
    rc_sent,
):
    z, x, c, y = position()
    barrier = pltpu.get_barrier_semaphore()
    for d in range(1, 4):
        pl.semaphore_signal(barrier, inc=1, device_id=device(z, x, c, (y + d) % 4), device_id_type=MESH)
        pl.semaphore_signal(barrier, inc=1, device_id=device((z + d) % 4, x, c, y), device_id_type=MESH)
    for dx, dc in OTHERS:
        pl.semaphore_signal(barrier, inc=1, device_id=device(z, (x + dx) % 4, (c + dc) % 2, y), device_id_type=MESH)

    for pair in range(2):
        for i in range(2):
            half = pl.ds(pl.multiple_of(64 * ((i + c) % 2), 64), 64)
            pltpu.make_async_copy(attn_grads.at[2 * pair + i], stack_attn.at[pair, half, :], grad_sem.at[0]).start()
    for i in range(2):
        half = pl.ds(pl.multiple_of(64 * ((i + c) % 2), 64), 64)
        pltpu.make_async_copy(mlp_grads.at[i], stack_mlp.at[0, half, :], grad_sem.at[1]).start()
        pltpu.make_async_copy(mlp_grads.at[2], stack_mlp.at[1, pl.ds(64 * i, 64), :], grad_sem.at[1]).start()
    for k, (attn, mlp) in enumerate(((attn_master, mlp_master), (attn_first, mlp_first), (attn_second, mlp_second))):

        def fetch(cb, carry, k=k, attn=attn, mlp=mlp):
            for m in range(4):
                pltpu.make_async_copy(attn.at[:, cb, m, :], state_attn.at[k, cb, m], state_sem.at[0]).start()
            for m in range(3):
                pltpu.make_async_copy(mlp.at[:, cb, m, :], state_mlp.at[k, cb, m], state_sem.at[1]).start()
            return carry

        lax.fori_loop(0, 16, fetch, 0)
    turned_mlp[1, pl.ds(1280, 8), :] = jnp.zeros((8, 128), F32)

    wait_for(stack_attn, grad_sem.at[0])
    wait_for(stack_mlp, grad_sem.at[1])

    def squares(value):
        return jnp.sum((value * value).reshape(-1, 8, value.shape[-1] // 128, 128), axis=(0, 2))

    total = jnp.zeros((8, 128), F32)
    for pair in range(2):
        for b in range(4):
            block = stack_attn[pair, :, b * 128 : (b + 1) * 128]
            total = total + jnp.sum((block * block).reshape(16, 8, 128), axis=0)
            turned_attn[pair, b * 128 : (b + 1) * 128, :] = block.T
    for b in range(10):
        block = stack_mlp[0, :, b * 128 : (b + 1) * 128]
        total = total + jnp.sum((block * block).reshape(16, 8, 128), axis=0)
        turned_mlp[0, b * 128 : (b + 1) * 128, :] = block.T
        block = stack_mlp[1, :, b * 128 : (b + 1) * 128]
        turned_mlp[1, b * 128 : (b + 1) * 128, :] = block.T
        block = block[:64]
        total = total + jnp.sum((block * block).reshape(8, 8, 128), axis=0)
    sums[0] = total

    straight = (low_lanes(24).astype(jnp.int32) + c) == 1

    def pack(xc, carry):
        for dest in range(4):
            j = xc * 4 + dest
            a_rows = pl.ds(pl.multiple_of(j * 16, 16), 16)
            m_rows = pl.ds(pl.multiple_of(j * 40, 8), 40)
            t_rows = pl.ds(pl.multiple_of(j * 40, 8), 24)
            u_rows = pl.ds(pl.multiple_of(j * 40 + 24, 8), 24)
            packed = jnp.concatenate(
                [
                    turned_attn[0, a_rows, :],
                    turned_attn[1, a_rows, :],
                    turned_mlp[0, m_rows, :],
                    jnp.where(straight, turned_mlp[1, t_rows, :], turned_mlp[1, u_rows, :]),
                ],
                axis=0,
            ).astype(BF16)
            da = (dest + 4 - y) % 4
            held[jnp.where(da == 0, 0, 3 + da), xc] = packed
        return carry

    lax.fori_loop(0, 8, pack, 0)

    pl.semaphore_wait(barrier, 13)

    def send_sum(src, slot, dev):
        pltpu.make_async_remote_copy(
            src_ref=sums.at[src],
            dst_ref=sums.at[slot],
            send_sem=sum_sent.at[slot],
            recv_sem=sum_recv.at[slot],
            device_id=dev,
            device_id_type=MESH,
        ).start()

    for d in range(1, 4):
        send_sum(0, 2 + d, device(z, x, c, (y + d) % 4))

    go = Exchange(True, held, landed, fa_recv, fb_recv, fc_recv, fa_sent, fb_sent, fc_sent)
    for da in (1, 3, 2):
        for xc in range(8):
            go.send_a(da, xc)
    go.pass_b(0)

    for slot in range(3, 6):
        wait_for(sums.at[slot], sum_recv.at[slot])
    sums[1] = sums[0] + sums[3] + sums[4] + sums[5]
    for k, (dx, dc) in enumerate(OTHERS):
        send_sum(1, 6 + k, device(z, (x + dx) % 4, (c + dc) % 2, y))

    go.pass_b(1)
    go.pass_c(0)

    for slot in range(6, 13):
        wait_for(sums.at[slot], sum_recv.at[slot])
    value = sums[1]
    for slot in range(6, 13):
        value = value + sums[slot]
    sums[2] = value
    for d in range(1, 4):
        send_sum(2, 12 + d, device((z + d) % 4, x, c, y))

    go.pass_b(3)
    go.pass_c(1)
    go.pass_b(2)
    go.pass_c(3)
    go.pass_c(2)

    for slot in range(13, 16):
        wait_for(sums.at[slot], sum_recv.at[slot])
    grand = jnp.sum(sums[2] + sums[13] + sums[14] + sums[15], keepdims=True)
    clip = jnp.minimum(1.0, clip_level / jnp.sqrt(grand / COUNT + 1e-06))
    clip_out[...] = jnp.broadcast_to(clip, (8, 128))

    wait_for(state_attn, state_sem.at[0])
    wait_for(state_mlp, state_sem.at[1])

    ret = Exchange(False, held_back, back, ra_recv, rb_recv, rc_recv, ra_sent, rb_sent, rc_sent)
    low = low_lanes(ROWS)

    def work(dz):
        source = (z + dz) % 4

        def one(xs, carry):
            if dz:
                go.take_c(source, xs * 2)
                go.take_c(source, xs * 2 + 1)
            cb = source * 4 + xs
            even, odd = split_halves(landed[source, xs * 2].astype(F32), landed[source, xs * 2 + 1].astype(F32))
            grads = (
                (flat_attn, state_attn, 0, 0, 16, even[0:16]),
                (flat_attn, state_attn, 2, 0, 16, even[16:32]),
                (flat_mlp, state_mlp, 0, 0, 40, even[32:72]),
                (flat_mlp, state_mlp, 2, 0, 24, even[72:96]),
                (flat_attn, state_attn, 1, 0, 16, odd[0:16]),
                (flat_attn, state_attn, 3, 0, 16, odd[16:32]),
                (flat_mlp, state_mlp, 1, 0, 40, odd[32:72]),
                (flat_mlp, state_mlp, 2, 24, 16, odd[72:88]),
            )
            new = []
            for flat, state, m, lo, n, g in grads:
                rows = pl.ds(lo, n)
                flat[cb, m, rows, :] = g
                new.append(
                    advance(g, state[0, cb, m, rows, :], state[1, cb, m, rows, :], state[2, cb, m, rows, :], clip)[0]
                )
            first_half = jnp.concatenate(new[:4], axis=0)
            other = pltpu.roll(jnp.concatenate(new[4:] + [jnp.zeros((8, 128), F32)], axis=0), 64, 1)
            place = 3 + dz if dz else 0
            held_back[place, xs * 2] = jnp.where(low, first_half, other).astype(BF16)
            held_back[place, xs * 2 + 1] = jnp.where(low, other, first_half).astype(BF16)
            for m in range(4):
                pltpu.make_async_copy(flat_attn.at[cb, m], attn_out.at[:, cb, m, :], flat_sem.at[0]).start()
            for m in range(3):
                pltpu.make_async_copy(flat_mlp.at[cb, m], mlp_out.at[:, cb, m, :], flat_sem.at[1]).start()
            if dz:
                ret.send_a(dz, xs * 2)
                ret.send_a(dz, xs * 2 + 1)
            return carry

        lax.fori_loop(0, 4, one, 0)

    work(0)
    ret.pass_b(0)
    work(1)
    work(3)
    ret.pass_b(1)
    work(2)
    ret.pass_b(3)
    ret.pass_c(0)
    ret.pass_b(2)
    ret.pass_c(1)
    ret.pass_c(3)
    ret.pass_c(2)
    for d in range(1, 4):
        for xc in range(8):
            ret.take_c((y + d) % 4, xc)

    go.drain()
    ret.drain()
    for slot in range(3, 16):
        wait_for(sums.at[slot], sum_sent.at[slot])
    wait_for(flat_attn, flat_sem.at[0])
    wait_for(flat_mlp, flat_sem.at[1])


def run_exchange(attn_grads, mlp_grads, states):
    dma = pltpu.SemaphoreType.DMA
    any_spec = pl.BlockSpec(memory_space=pl.ANY)
    return pl.pallas_call(
        exchange_kernel,
        name="exchange",
        out_shape=(
            jax.ShapeDtypeStruct((16, 16, 4, 128), F32),
            jax.ShapeDtypeStruct((40, 16, 3, 128), F32),
            jax.ShapeDtypeStruct((8, 128), F32),
            jax.ShapeDtypeStruct((8, 8, ROWS, 128), BF16),
        ),
        in_specs=[any_spec] * 8,
        out_specs=(any_spec, any_spec, pl.BlockSpec(memory_space=pltpu.VMEM), any_spec),
        scratch_shapes=[
            pltpu.VMEM((2, 128, 512), F32),
            pltpu.VMEM((2, 128, 1280), F32),
            pltpu.VMEM((2, 512, 128), F32),
            pltpu.VMEM((2, 1288, 128), F32),
            pltpu.VMEM((7, 8, ROWS, 128), BF16),
            pltpu.VMEM((8, 8, ROWS, 128), BF16),
            pltpu.VMEM((7, 8, ROWS, 128), BF16),
            pltpu.VMEM((3, 16, 4, 16, 128), F32),
            pltpu.VMEM((3, 16, 3, 40, 128), F32),
            pltpu.VMEM((16, 4, 16, 128), F32),
            pltpu.VMEM((16, 3, 40, 128), F32),
            pltpu.VMEM((16, 8, 128), F32),
            dma((2,)),
            dma((2,)),
            dma((2,)),
            dma((16,)),
            dma((16,)),
            dma((4, 8)),
            dma((4, 8)),
            dma((4, 8)),
            dma,
            dma((4,)),
            dma,
            dma((4, 8)),
            dma((4, 8)),
            dma((4, 8)),
            dma,
            dma((4,)),
            dma,
        ],
        compiler_params=pltpu.CompilerParams(collective_id=0, has_side_effects=True, vmem_limit_bytes=32 << 20),
    )(attn_grads, mlp_grads, *states)


def rows_first(flat, rows):
    return flat.reshape(flat.shape[0], rows, 16, 128).transpose(1, 2, 0, 3)


def members_first(value):
    rows, _, members, _ = value.shape
    return value.transpose(2, 0, 1, 3).reshape(members, rows * D)


def per_device(
    attn_grads,
    mlp_grads,
    attn_master,
    attn_first,
    attn_second,
    attn_average,
    mlp_master,
    mlp_first,
    mlp_second,
    mlp_average,
):
    attn_states = [rows_first(v, 16) for v in (attn_master, attn_first, attn_second)]
    mlp_states = [rows_first(v, 40) for v in (mlp_master, mlp_first, mlp_second)]
    flat_attn, flat_mlp, clip, back = run_exchange(
        attn_grads.transpose(0, 2, 1), mlp_grads.transpose(0, 2, 1), attn_states + mlp_states
    )
    factor = clip[0, 0]
    outs = []
    for grads, master, first, second, average in (
        (members_first(flat_attn), attn_master, attn_first, attn_second, attn_average),
        (members_first(flat_mlp), mlp_master, mlp_first, mlp_second, mlp_average),
    ):
        master_new, first_new, second_new = advance(grads, master, first, second, factor)
        outs += [master_new, first_new, second_new, average_keep * average + (1.0 - average_keep) * master_new]

    chunks = back[:4].transpose(1, 0, 2, 3).reshape(32, ROWS, 128)
    swapped = lax.axis_index("shard") % 2 == 1
    left, right = chunks[:, :, :64], chunks[:, :, 64:]
    even = jnp.where(swapped, right, left)
    odd = jnp.where(swapped, left, right)
    attn_weights = jnp.stack(
        [
            even[:, 0:16].reshape(512, 64),
            odd[:, 0:16].reshape(512, 64),
            even[:, 16:32].reshape(512, 64),
            odd[:, 16:32].reshape(512, 64),
        ]
    )
    mlp_weights = jnp.stack(
        [
            even[:, 32:72].reshape(1280, 64),
            odd[:, 32:72].reshape(1280, 64),
            jnp.concatenate([even[:, 72:96], odd[:, 72:88]], axis=1).reshape(1280, 64),
        ]
    )
    return (*outs, attn_weights, mlp_weights)


def solution(mesh):
    whole = P(None, "tensor", "shard")
    flat = P(None, ("shard", "tensor"))
    return jax.shard_map(
        per_device,
        mesh=mesh,
        in_specs=(whole,) * 2 + (flat,) * 8,
        out_specs=(flat,) * 8 + (whole,) * 2,
        check_vma=False,
    )
```

time: 202 us -> 91.6 us (0.45)
  blocking collectives: 63.1 us -> 0 us
  Pallas kernels: 0 us -> 62.6 us
  starting transfers between devices: 43.2 us -> 0 us
  waiting for transfers between devices: 38.3 us -> 0 us
  local copies, waits for them, and re-layouts: 39.2 us -> 14.9 us
  between operations: 3 us -> 0.78 us
    psum x1 -> x0, blocking collectives: 63.1 us -> none  [total_squares(): lax.psum((jnp.sum(first_part * first_part), jnp.sum(second_part * second_...]
    pallas_call x0 -> x1, Pallas kernels: none -> 62.6 us  [run_exchange(): pl.pallas_call(exchange_kernel, name='exchange', out_shape=(jax.ShapeDtyp...]
    all_to_all x8 -> x0, starting transfers between devices: 43.2 us -> none  [the longest x1 11.2 us: per_device(): lax.all_to_all(by_shard(sectioned_attn).astype(jnp.bfloat16), 'shard', sp...]
    all_to_all x8 -> x0, waiting for transfers between devices: 38.3 us -> none  [the longest x1 10.1 us: per_device(): lax.all_to_all(by_shard(sectioned_mlp).astype(jnp.bfloat16), 'shard', spl...]
    unnamed x38 -> x32, local copies, waits for them, and re-layouts: 25.6 us -> 13.4 us
    convert_element_type x2 -> x0, other arithmetic: 6.92 us -> none  [to_return(): master_new.astype(jnp.bfloat16).reshape(member_count, 1, piece_rows, D)]
    mul x4 -> x0, local copies, waits for them, and re-layouts: 6.07 us -> none  [advance(): clipped = clip_factor * flat_grads]
    reshape x4 -> x0, local copies, waits for them, and re-layouts: 4.17 us -> none  [the longest x2 4.04 us: to_return(): master_new.astype(jnp.bfloat16).reshape(member_count, 1, piece_rows, D)]
  transfers between devices with their start and end apart: 8 -> 0, of which waited for: 6 -> 0; matrix products, arithmetic and copies ran while one was open for 16% -> 0% of each run, Pallas kernels for 0% -> 0%
where the time goes in v1:
time: 91.6 us; the launch traced here: 90.1 us
  Pallas kernels  62.6 us (68%)
  local copies, waits for them, and re-layouts  14.9 us (16%)
  other arithmetic  11.8 us (13%)
    pallas_call x1, Pallas kernels, run_exchange(): pl.pallas_call(exchange_kernel, name='exchange', out_shape=(jax.ShapeDtyp...  62.6 us
    unnamed x32, local copies, waits for them, and re-layouts  13.4 us
    add x2, other arithmetic, per_device(): average_keep * average + (1.0 - average_keep) * master_new  7.46 us
    another operation x1, other arithmetic, per_device(): jnp.stack([even[:, 0:16].reshape(512, 64), odd[:, 0:16].reshape(512, 64),...  1.95 us

profile of v1, /device:TPU:1, one launch (start us, length us, event | category | flops | bytes accessed | tf_op | source)
XLA Modules:
  0.0 90.1 jit_solution(14618507154538094731)
XLA Ops:
  0.7 0.0 copy-start
  0.7 1.3 %copy-done = f32[3,81920]{1,0:T(4,128)S(1)} copy-done((f32[3,81920]{1,0:T(4,128)S(1)}, f32[3,81920]{1,0:T(4,128)}, u32[]{:S(2)}) %copy-start) | copy-done | bytes 983064
  2.0 0.0 copy-start.2
  2.0 1.3 %copy-done.2 = f32[3,81920]{1,0:T(4,128)S(1)} copy-done((f32[3,81920]{1,0:T(4,128)S(1)}, f32[3,81920]{1,0:T(4,128)}, u32[]{:S(2)}) %copy-start.2) | copy-done | bytes 983064
  3.3 0.0 copy-start.4
  3.3 1.3 %copy-done.4 = f32[3,81920]{1,0:T(4,128)S(1)} copy-done((f32[3,81920]{1,0:T(4,128)S(1)}, f32[3,81920]{1,0:T(4,128)}, u32[]{:S(2)}) %copy-start.4) | copy-done | bytes 983064
  4.6 0.0 copy-start.6
  4.6 1.0 %copy-done.6 = f32[4,32768]{1,0:T(4,128)S(1)} copy-done((f32[4,32768]{1,0:T(4,128)S(1)}, f32[4,32768]{1,0:T(4,128)}, u32[]{:S(2)}) %copy-start.6) | copy-done | bytes 524312
  5.7 0.0 copy-start.8
  5.7 1.0 %copy-done.8 = f32[4,32768]{1,0:T(4,128)S(1)} copy-done((f32[4,32768]{1,0:T(4,128)S(1)}, f32[4,32768]{1,0:T(4,128)}, u32[]{:S(2)}) %copy-start.8) | copy-done | bytes 524312
  6.7 0.0 copy-start.10
  6.7 1.0 %copy-done.10 = f32[4,32768]{1,0:T(4,128)S(1)} copy-done((f32[4,32768]{1,0:T(4,128)S(1)}, f32[4,32768]{1,0:T(4,128)}, u32[]{:S(2)}) %copy-start.10) | copy-done | bytes 524312
  7.7 0.0 copy-start.12
  7.7 1.2 %copy-done.12 = f32[3,1280,64]{1,2,0:T(8,128)S(1)} copy-done((f32[3,1280,64]{1,2,0:T(8,128)S(1)}, f32[3,1280,64]{1,2,0:T(8,128)}, u32[]{:S(2)}) %copy-start.12) | copy-done | bytes 983064
  8.9 0.0 copy-start.13
  8.9 1.0 %copy-done.13 = f32[4,512,64]{1,2,0:T(8,128)S(1)} copy-done((f32[4,512,64]{1,2,0:T(8,128)S(1)}, f32[4,512,64]{1,2,0:T(8,128)}, u32[]{:S(2)}) %copy-start.13) | copy-done | bytes 524312
  10.0 62.6 %exchange.1 = (f32[16,16,4,128]{3,2,1,0:T(4,128)S(1)}, f32[40,16,3,128]{3,2,1,0:T(4,128)S(1)}, f32[8,128]{1,0:T(8,128)S(1)}, bf16[8,8,96,128]{3,2,1,0:T(8,128)(2,1)S(1)}) custom-call(f32[4,64,512]{2,1,0:T(8,128)S(1)} %bitcast.47, f32[3,64,1280]{2,1,0:T(8,128)S(1)} %bitcast.45, f32[16,16,4,128]{3,2,1,0:T(4,128)S(1)} %bitcast.42, ...), custom_call_target="tpu_custom_call" | custom-call | tf_op jit(solution)/shard_map/exchange/pallas_call | solution.py:384
  72.6 0.1 slice_bitcast_fusion
  72.7 0.1 copy.20
  72.7 0.3 broadcast_select_fusion.1
  73.0 0.8 fusion.4
  73.8 0.1 pad_maximum_fusion.2
  74.0 0.2 pad_maximum_fusion
  74.2 1.1 %copy.22 = bf16[3,1280,64]{1,2,0:T(8,128)(2,1)} copy(bf16[3,1280,64]{2,1,0:T(8,128)(2,1)S(1)} %pad_maximum_fusion) | data formatting | bytes 983040
  75.3 0.0 copy-start.5
  75.3 1.9 %pad_maximum_fusion.1 = bf16[4,512,64]{2,1,0:T(8,128)(2,1)} fusion(bf16[1,512,64]{2,1,0:T(8,128)(2,1)S(1)} %bitcast.54, bf16[1,512,64]{2,1,0:T(8,128)(2,1)S(1)} %bitcast.56, bf16[1,512,64]{2,1,0:T(8,128)(2,1)S(1)} %bitcast.55, bf16[1,512,64]{2,1,0:T(8,128)(2,1)} %bitcast.57), kind=kLoop, calls=%fused_computation.12 | loop fusion | flops 393216 | bytes 524288 | tf_op jit(solution)/shard_map/stack | solution.py:470
  77.3 1.9 %copy.21 = bf16[4,512,64]{1,2,0:T(8,128)(2,1)} copy(bf16[4,512,64]{2,1,0:T(8,128)(2,1)} %pad_maximum_fusion.1) | data formatting | bytes 524288
  79.2 0.5 slice.36
  79.7 0.0 copy-start.1
  79.7 0.0 copy-start.3
  79.7 1.1 %broadcast_multiply_fusion = f32[40,16,3,128]{3,2,1,0:T(4,128)S(1)} fusion(f32[40,16,3,128]{3,2,1,0:T(4,128)S(1)} %get-tuple-element.16, f32[]{:T(128)} %bitcast.14), kind=kLoop, calls=%fused_computation.10 | loop fusion | flops 245760 | bytes 1966084 | tf_op jit(solution)/shard_map/mul | solution.py:29
  80.8 0.0 copy-done.5
  80.8 0.3 copy-done.1
  81.1 0.4 copy-done.3
  81.5 0.0 copy-start.11
  81.5 0.0 copy-start.14
  81.5 5.2 %multiply_add_fusion = (f32[3,81920]{1,0:T(4,128)}, f32[3,81920]{1,0:T(4,128)}, f32[3,81920]{1,0:T(4,128)}, f32[3,81920]{1,0:T(4,128)}) fusion(f32[3,81920]{1,0:T(4,128)} %param.19, f32[3,81920]{1,0:T(4,128)S(1)} %copy-done.1, f32[3,81920]{1,0:T(4,128)S(1)} %bitcast.49, f32[3,81920]{1,0:T(4,128)S(1)} %copy-done.3, f32[3,81920]{1,0:T(4,128)S(1)} %copy-done.5), kind=kLoop, calls=%fused_computation.2 | loop fusion | flops 4423680 | bytes 8847360 | tf_op jit(solution)/shard_map/add | solution.py:463
  86.7 0.0 copy-start.7
  86.7 0.0 copy-start.9
  86.7 0.8 broadcast_multiply_fusion.1
  87.5 0.0 copy-done.11
  87.5 0.0 copy-done.14
  87.5 0.2 copy-done.7
  87.8 0.2 copy-done.9
  87.9 2.2 %multiply_add_fusion.2 = (f32[4,32768]{1,0:T(4,128)}, f32[4,32768]{1,0:T(4,128)}, f32[4,32768]{1,0:T(4,128)}, f32[4,32768]{1,0:T(4,128)}) fusion(f32[4,32768]{1,0:T(4,128)S(1)} %copy-done.14, f32[4,32768]{1,0:T(4,128)S(1)} %copy-done.7, f32[4,32768]{1,0:T(4,128)S(1)} %bitcast.50, f32[4,32768]{1,0:T(4,128)S(1)} %copy-done.9, f32[4,32768]{1,0:T(4,128)S(1)} %copy-done.11), kind=kLoop, calls=%fused_computation.13 | loop fusion | flops 2359296 | bytes 4718592 | tf_op jit(solution)/shard_map/add | solution.py:463
  (3 shorter events, 0.1 us)
Async XLA Ops:
  0.7 1.3 %copy-start = (f32[3,81920]{1,0:T(4,128)S(1)}, f32[3,81920]{1,0:T(4,128)}, u32[]{:S(2)}) copy-start(f32[3,81920]{1,0:T(4,128)} %param.16) | copy-start | bytes 2949124
  2.0 1.3 %copy-start.2 = (f32[3,81920]{1,0:T(4,128)S(1)}, f32[3,81920]{1,0:T(4,128)}, u32[]{:S(2)}) copy-start(f32[3,81920]{1,0:T(4,128)} %param.17) | copy-start | bytes 2949124
  3.3 1.3 %copy-start.4 = (f32[3,81920]{1,0:T(4,128)S(1)}, f32[3,81920]{1,0:T(4,128)}, u32[]{:S(2)}) copy-start(f32[3,81920]{1,0:T(4,128)} %param.18) | copy-start | bytes 2949124
  4.6 1.0 %copy-start.6 = (f32[4,32768]{1,0:T(4,128)S(1)}, f32[4,32768]{1,0:T(4,128)}, u32[]{:S(2)}) copy-start(f32[4,32768]{1,0:T(4,128)} %param.12) | copy-start | bytes 1572868
  5.7 1.0 %copy-start.8 = (f32[4,32768]{1,0:T(4,128)S(1)}, f32[4,32768]{1,0:T(4,128)}, u32[]{:S(2)}) copy-start(f32[4,32768]{1,0:T(4,128)} %param.13) | copy-start | bytes 1572868
  6.7 1.0 %copy-start.10 = (f32[4,32768]{1,0:T(4,128)S(1)}, f32[4,32768]{1,0:T(4,128)}, u32[]{:S(2)}) copy-start(f32[4,32768]{1,0:T(4,128)} %param.14) | copy-start | bytes 1572868
  7.7 1.2 %copy-start.12 = (f32[3,1280,64]{1,2,0:T(8,128)S(1)}, f32[3,1280,64]{1,2,0:T(8,128)}, u32[]{:S(2)}) copy-start(f32[3,1280,64]{1,2,0:T(8,128)} %param.11) | copy-start | bytes 2949124
  8.9 1.0 %copy-start.13 = (f32[4,512,64]{1,2,0:T(8,128)S(1)}, f32[4,512,64]{1,2,0:T(8,128)}, u32[]{:S(2)}) copy-start(f32[4,512,64]{1,2,0:T(8,128)} %param.10) | copy-start | bytes 1572868
  75.3 5.5 %copy-start.5 = (f32[3,81920]{1,0:T(4,128)S(1)}, f32[3,81920]{1,0:T(4,128)}, u32[]{:S(2)}) copy-start(f32[3,81920]{1,0:T(4,128)} %param.18) | copy-start | bytes 2949124
  79.7 1.3 %copy-start.1 = (f32[3,81920]{1,0:T(4,128)S(1)}, f32[3,81920]{1,0:T(4,128)}, u32[]{:S(2)}) copy-start(f32[3,81920]{1,0:T(4,128)} %param.16) | copy-start | bytes 2949124
  79.7 1.7 %copy-start.3 = (f32[3,81920]{1,0:T(4,128)S(1)}, f32[3,81920]{1,0:T(4,128)}, u32[]{:S(2)}) copy-start(f32[3,81920]{1,0:T(4,128)} %param.17) | copy-start | bytes 2949124
  81.5 6.0 %copy-start.11 = (f32[4,32768]{1,0:T(4,128)S(1)}, f32[4,32768]{1,0:T(4,128)}, u32[]{:S(2)}) copy-start(f32[4,32768]{1,0:T(4,128)} %param.14) | copy-start | bytes 1572868
  81.5 6.0 %copy-start.14 = (f32[4,32768]{1,0:T(4,128)S(1)}, f32[4,32768]{1,0:T(4,128)}, u32[]{:S(2)}) copy-start(f32[4,32768]{1,0:T(4,128)} %param.15) | copy-start | bytes 1572868
  86.7 1.1 %copy-start.7 = (f32[4,32768]{1,0:T(4,128)S(1)}, f32[4,32768]{1,0:T(4,128)}, u32[]{:S(2)}) copy-start(f32[4,32768]{1,0:T(4,128)} %param.12) | copy-start | bytes 1572868
  86.7 1.2 %copy-start.9 = (f32[4,32768]{1,0:T(4,128)S(1)}, f32[4,32768]{1,0:T(4,128)}, u32[]{:S(2)}) copy-start(f32[4,32768]{1,0:T(4,128)} %param.13) | copy-start | bytes 1572868

commit v2 on v1

v2 whole, which is shorter than its diff:
```python
import functools

import jax
import jax.numpy as jnp
from jax import lax
from jax.experimental import pallas as pl
from jax.experimental.pallas import tpu as pltpu
from jax.sharding import PartitionSpec as P

D = 2048
STEP = 100
COUNT = 48234496

beta_one = 0.9
beta_two = 0.999
adam_eps = 1e-08
learn_rate = 0.01
decay_weight = 0.1
average_keep = 0.999
clip_level = 1.0

MESH = pl.DeviceIdType.MESH
ROWS = 96
F32 = jnp.float32
BF16 = jnp.bfloat16


def advance(grads, master, first, second, average, clip):
    clipped = clip * grads
    first_new = beta_one * first + (1.0 - beta_one) * clipped
    second_new = beta_two * second + (1.0 - beta_two) * clipped * clipped
    update = (first_new * (1.0 / (1.0 - beta_one**STEP))) / (
        jnp.sqrt(second_new * (1.0 / (1.0 - beta_two**STEP))) + adam_eps
    )
    master_new = master - learn_rate * (update + decay_weight * master)
    average_new = average_keep * average + (1.0 - average_keep) * master_new
    return master_new, first_new, second_new, average_new


def low_lanes(rows):
    return lax.broadcasted_iota(jnp.int32, (rows, 128), 1) < 64


def split_halves(p_zero, p_one):
    low = low_lanes(p_zero.shape[0])
    return jnp.where(low, p_zero, p_one), pltpu.roll(jnp.where(low, p_one, p_zero), 64, 1)


def position():
    s = lax.axis_index("shard")
    return s // 8, (s // 2) % 4, s % 2, lax.axis_index("tensor")


def device(z, x, c, y):
    return (z * 8 + x * 2 + c, y)


def wait_for(ref, sem):
    pltpu.make_async_copy(ref, ref, sem).wait()


OTHERS = [(dx, dc) for dx in range(4) for dc in range(2)][1:]
TURNS = (1, 3, 2, 0)
RING = (0, 1, 3, 2)


class Exchange:
    def __init__(self, forward, held, landed, a_recv, b_recv, c_recv, a_sent, b_sent, c_sent):
        self.held, self.landed = held, landed
        self.a_recv, self.b_recv, self.c_recv = a_recv, b_recv, c_recv
        self.a_sent, self.b_sent, self.c_sent = a_sent, b_sent, c_sent
        self.z, self.x, self.c, self.y = position()
        self.forward = forward
        self.a, self.b = (self.y, self.z) if forward else (self.z, self.y)
        self.mine = self.x * 2 + self.c

    def at(self, a, x, c, b):
        return device(b, x, c, a) if self.forward else device(a, x, c, b)

    def target(self, turn, dc):
        dx = TURNS[turn] if self.forward else (4 - TURNS[turn]) % 4
        return (self.x + dx) % 4, (self.c + dc) % 2

    def source(self, turn, dc):
        dx = TURNS[turn] if self.forward else (4 - TURNS[turn]) % 4
        return (self.x + 4 - dx) % 4, (self.c + dc) % 2

    def send_a(self, da, xc):
        pltpu.make_async_remote_copy(
            src_ref=self.held.at[3 + da, xc],
            dst_ref=self.held.at[da, xc],
            send_sem=self.a_sent,
            recv_sem=self.a_recv.at[da, xc],
            device_id=self.at((self.a + da) % 4, self.x, self.c, self.b),
            device_id_type=MESH,
        ).start()

    def origin(self, da):
        origin = (self.a + 4 - da) % 4
        return origin, jnp.where(origin == self.b, origin, 4 + origin)

    def pass_b(self, turn):
        for dc in range(2):
            x, c = self.target(turn, dc)
            xc = x * 2 + c
            for da in RING:
                origin, slot = self.origin(da)
                if da:
                    wait_for(self.held.at[da, xc], self.a_recv.at[da, xc])
                if TURNS[turn] or dc:
                    pltpu.make_async_remote_copy(
                        src_ref=self.held.at[da, xc],
                        dst_ref=self.landed.at[slot, self.mine],
                        send_sem=self.b_sent.at[da],
                        recv_sem=self.b_recv.at[origin, self.mine],
                        device_id=self.at(self.a, x, c, self.b),
                        device_id_type=MESH,
                    ).start()
                else:
                    pltpu.make_async_copy(
                        self.held.at[da, xc], self.landed.at[slot, xc], self.b_recv.at[origin, xc]
                    ).start()

    def pass_c(self, turn):
        for dc in range(2):
            x, c = self.source(turn, dc)
            xc = x * 2 + c
            for da in RING:
                origin, slot = self.origin(da)
                wait_for(self.landed.at[slot, xc], self.b_recv.at[origin, xc])

                @pl.when(origin != self.b)
                def _():
                    pltpu.make_async_remote_copy(
                        src_ref=self.landed.at[slot, xc],
                        dst_ref=self.landed.at[self.b, xc],
                        send_sem=self.c_sent,
                        recv_sem=self.c_recv.at[self.b, xc],
                        device_id=self.at(self.a, self.x, self.c, origin),
                        device_id_type=MESH,
                    ).start()

    def take_c(self, source, xc):
        wait_for(self.landed.at[source, xc], self.c_recv.at[source, xc])

    def drain(self):
        wait_for(self.held.at[pl.ds(4, 3)], self.a_sent)
        for da in range(4):
            wait_for(self.held.at[da, pl.ds(0, 7)], self.b_sent.at[da])
        wait_for(self.held.at[pl.ds(4, 3)], self.c_sent)


def exchange_kernel(
    attn_grads,
    mlp_grads,
    attn_master,
    attn_first,
    attn_second,
    attn_average,
    mlp_master,
    mlp_first,
    mlp_second,
    mlp_average,
    attn_master_new,
    attn_first_new,
    attn_second_new,
    attn_average_new,
    mlp_master_new,
    mlp_first_new,
    mlp_second_new,
    mlp_average_new,
    back,
    stack_attn,
    stack_mlp,
    turned_attn,
    turned_mlp,
    held,
    landed,
    held_back,
    state_attn,
    state_mlp,
    sums,
    grad_sem,
    state_sem,
    flat_sem,
    sum_recv,
    sum_sent,
    fa_recv,
    fb_recv,
    fc_recv,
    fa_sent,
    fb_sent,
    fc_sent,
    ra_recv,
    rb_recv,
    rc_recv,
    ra_sent,
    rb_sent,
    rc_sent,
):
    z, x, c, y = position()
    barrier = pltpu.get_barrier_semaphore()
    for d in range(1, 4):
        pl.semaphore_signal(barrier, inc=1, device_id=device(z, x, c, (y + d) % 4), device_id_type=MESH)
        pl.semaphore_signal(barrier, inc=1, device_id=device((z + d) % 4, x, c, y), device_id_type=MESH)
    for dx, dc in OTHERS:
        pl.semaphore_signal(barrier, inc=1, device_id=device(z, (x + dx) % 4, (c + dc) % 2, y), device_id_type=MESH)

    for pair in range(2):
        for i in range(2):
            half = pl.ds(pl.multiple_of(64 * ((i + c) % 2), 64), 64)
            pltpu.make_async_copy(attn_grads.at[2 * pair + i], stack_attn.at[pair, half, :], grad_sem.at[0]).start()
    for i in range(2):
        half = pl.ds(pl.multiple_of(64 * ((i + c) % 2), 64), 64)
        pltpu.make_async_copy(mlp_grads.at[i], stack_mlp.at[0, half, :], grad_sem.at[1]).start()
        pltpu.make_async_copy(mlp_grads.at[2], stack_mlp.at[1, pl.ds(64 * i, 64), :], grad_sem.at[1]).start()
    olds = (
        (attn_master, mlp_master),
        (attn_first, mlp_first),
        (attn_second, mlp_second),
        (attn_average, mlp_average),
    )
    for k, (attn, mlp) in enumerate(olds):

        def fetch(cb, carry, k=k, attn=attn, mlp=mlp):
            for m in range(4):
                pltpu.make_async_copy(attn.at[:, cb, m, :], state_attn.at[k, cb, m], state_sem.at[0]).start()
            for m in range(3):
                pltpu.make_async_copy(mlp.at[:, cb, m, :], state_mlp.at[k, cb, m], state_sem.at[1]).start()
            return carry

        lax.fori_loop(0, 16, fetch, 0)
    turned_mlp[1, pl.ds(1280, 8), :] = jnp.zeros((8, 128), F32)

    wait_for(stack_attn, grad_sem.at[0])
    wait_for(stack_mlp, grad_sem.at[1])

    total = jnp.zeros((8, 128), F32)
    for pair in range(2):
        for b in range(4):
            block = stack_attn[pair, :, b * 128 : (b + 1) * 128]
            total = total + jnp.sum((block * block).reshape(16, 8, 128), axis=0)
            turned_attn[pair, b * 128 : (b + 1) * 128, :] = block.T
    for b in range(10):
        block = stack_mlp[0, :, b * 128 : (b + 1) * 128]
        total = total + jnp.sum((block * block).reshape(16, 8, 128), axis=0)
        turned_mlp[0, b * 128 : (b + 1) * 128, :] = block.T
        block = stack_mlp[1, :, b * 128 : (b + 1) * 128]
        turned_mlp[1, b * 128 : (b + 1) * 128, :] = block.T
        block = block[:64]
        total = total + jnp.sum((block * block).reshape(8, 8, 128), axis=0)
    sums[0] = total

    straight = (low_lanes(24).astype(jnp.int32) + c) == 1

    def pack(xc, carry):
        for dest in range(4):
            j = xc * 4 + dest
            a_rows = pl.ds(pl.multiple_of(j * 16, 16), 16)
            m_rows = pl.ds(pl.multiple_of(j * 40, 8), 40)
            t_rows = pl.ds(pl.multiple_of(j * 40, 8), 24)
            u_rows = pl.ds(pl.multiple_of(j * 40 + 24, 8), 24)
            packed = jnp.concatenate(
                [
                    turned_attn[0, a_rows, :],
                    turned_attn[1, a_rows, :],
                    turned_mlp[0, m_rows, :],
                    jnp.where(straight, turned_mlp[1, t_rows, :], turned_mlp[1, u_rows, :]),
                ],
                axis=0,
            ).astype(BF16)
            da = (dest + 4 - y) % 4
            held[jnp.where(da == 0, 0, 3 + da), xc] = packed
        return carry

    lax.fori_loop(0, 8, pack, 0)

    pl.semaphore_wait(barrier, 13)

    def send_sum(src, slot, dev):
        pltpu.make_async_remote_copy(
            src_ref=sums.at[src],
            dst_ref=sums.at[slot],
            send_sem=sum_sent.at[slot],
            recv_sem=sum_recv.at[slot],
            device_id=dev,
            device_id_type=MESH,
        ).start()

    for d in range(1, 4):
        send_sum(0, 2 + d, device(z, x, c, (y + d) % 4))

    go = Exchange(True, held, landed, fa_recv, fb_recv, fc_recv, fa_sent, fb_sent, fc_sent)
    for turn in range(4):
        for dc in range(2):
            tx, tc = go.target(turn, dc)
            for da in RING[1:]:
                go.send_a(da, tx * 2 + tc)
    go.pass_b(0)

    for slot in range(3, 6):
        wait_for(sums.at[slot], sum_recv.at[slot])
    sums[1] = sums[0] + sums[3] + sums[4] + sums[5]
    for k, (dx, dc) in enumerate(OTHERS):
        send_sum(1, 6 + k, device(z, (x + dx) % 4, (c + dc) % 2, y))

    go.pass_b(1)
    go.pass_c(0)

    for slot in range(6, 13):
        wait_for(sums.at[slot], sum_recv.at[slot])
    value = sums[1]
    for slot in range(6, 13):
        value = value + sums[slot]
    sums[2] = value
    for d in range(1, 4):
        send_sum(2, 12 + d, device((z + d) % 4, x, c, y))

    go.pass_b(2)
    go.pass_c(1)
    go.pass_b(3)
    go.pass_c(2)

    for slot in range(13, 16):
        wait_for(sums.at[slot], sum_recv.at[slot])
    grand = jnp.sum(sums[2] + sums[13] + sums[14] + sums[15], keepdims=True)
    clip = jnp.minimum(1.0, clip_level / jnp.sqrt(grand / COUNT + 1e-06))

    wait_for(state_attn, state_sem.at[0])
    wait_for(state_mlp, state_sem.at[1])

    ret = Exchange(False, held_back, back, ra_recv, rb_recv, rc_recv, ra_sent, rb_sent, rc_sent)
    low = low_lanes(ROWS)

    def work(turn):
        xs, _ = go.source(turn, 0)

        def one(source, place, da):
            cb = source * 4 + xs
            even, odd = split_halves(landed[source, xs * 2].astype(F32), landed[source, xs * 2 + 1].astype(F32))
            pieces = (
                (state_attn, 0, 0, 16, even[0:16]),
                (state_attn, 2, 0, 16, even[16:32]),
                (state_mlp, 0, 0, 40, even[32:72]),
                (state_mlp, 2, 0, 24, even[72:96]),
                (state_attn, 1, 0, 16, odd[0:16]),
                (state_attn, 3, 0, 16, odd[16:32]),
                (state_mlp, 1, 0, 40, odd[32:72]),
                (state_mlp, 2, 24, 16, odd[72:88]),
            )
            new = []
            for state, m, lo, n, g in pieces:
                rows = pl.ds(lo, n)
                values = advance(g, *(state[k, cb, m, rows, :] for k in range(4)), clip)
                for k in range(4):
                    state[k, cb, m, rows, :] = values[k]
                new.append(values[0])
            first_half = jnp.concatenate(new[:4], axis=0)
            other = pltpu.roll(jnp.concatenate(new[4:] + [jnp.zeros((8, 128), F32)], axis=0), 64, 1)
            held_back[place, xs * 2] = jnp.where(low, first_half, other).astype(BF16)
            held_back[place, xs * 2 + 1] = jnp.where(low, other, first_half).astype(BF16)

        one(z, 0, 0)

        def distant(da, carry):
            source = (z + da) % 4
            for dc in range(2):
                go.take_c(source, xs * 2 + dc)
            one(source, 3 + da, da)
            for dc in range(2):
                ret.send_a(da, xs * 2 + dc)
            return carry

        lax.fori_loop(1, 4, distant, 0)

    news = (
        (attn_master_new, mlp_master_new),
        (attn_first_new, mlp_first_new),
        (attn_second_new, mlp_second_new),
        (attn_average_new, mlp_average_new),
    )

    def store(turn):
        xs, _ = go.source(turn, 0)

        def one(zs, carry):
            cb = zs * 4 + xs
            for k, (attn, mlp) in enumerate(news):
                for m in range(4):
                    pltpu.make_async_copy(state_attn.at[k, cb, m], attn.at[:, cb, m, :], flat_sem.at[0]).start()
                for m in range(3):
                    pltpu.make_async_copy(state_mlp.at[k, cb, m], mlp.at[:, cb, m, :], flat_sem.at[1]).start()
            return carry

        lax.fori_loop(0, 4, one, 0)

    work(0)
    work(1)
    ret.pass_b(0)
    go.pass_c(3)
    work(2)
    ret.pass_b(1)
    ret.pass_c(0)
    work(3)
    ret.pass_b(2)
    ret.pass_c(1)
    ret.pass_b(3)
    store(0)
    ret.pass_c(2)
    store(1)
    ret.pass_c(3)
    store(2)
    store(3)
    for d in range(1, 4):
        for xc in range(8):
            ret.take_c((y + d) % 4, xc)

    go.drain()
    ret.drain()
    for slot in range(3, 16):
        wait_for(sums.at[slot], sum_sent.at[slot])
    wait_for(state_attn, flat_sem.at[0])
    wait_for(state_mlp, flat_sem.at[1])


def run_exchange(args):
    dma = pltpu.SemaphoreType.DMA
    any_spec = pl.BlockSpec(memory_space=pl.ANY)
    return pl.pallas_call(
        exchange_kernel,
        name="exchange",
        out_shape=(
            *[jax.ShapeDtypeStruct((16, 16, 4, 128), F32)] * 4,
            *[jax.ShapeDtypeStruct((40, 16, 3, 128), F32)] * 4,
            jax.ShapeDtypeStruct((8, 8, ROWS, 128), BF16),
        ),
        in_specs=[pl.BlockSpec(memory_space=pltpu.HBM)] * 10,
        out_specs=[any_spec] * 9,
        scratch_shapes=[
            pltpu.VMEM((2, 128, 512), F32),
            pltpu.VMEM((2, 128, 1280), F32),
            pltpu.VMEM((2, 512, 128), F32),
            pltpu.VMEM((2, 1288, 128), F32),
            pltpu.VMEM((7, 8, ROWS, 128), BF16),
            pltpu.VMEM((8, 8, ROWS, 128), BF16),
            pltpu.VMEM((7, 8, ROWS, 128), BF16),
            pltpu.VMEM((4, 16, 4, 16, 128), F32),
            pltpu.VMEM((4, 16, 3, 40, 128), F32),
            pltpu.VMEM((16, 8, 128), F32),
            dma((2,)),
            dma((2,)),
            dma((2,)),
            dma((16,)),
            dma((16,)),
            dma((4, 8)),
            dma((4, 8)),
            dma((4, 8)),
            dma,
            dma((4,)),
            dma,
            dma((4, 8)),
            dma((4, 8)),
            dma((4, 8)),
            dma,
            dma((4,)),
            dma,
        ],
        compiler_params=pltpu.CompilerParams(collective_id=0, has_side_effects=True, vmem_limit_bytes=32 << 20),
    )(*args)


def finish_kernel(*refs):
    news, back, outs = refs[:8], refs[8], refs[9:17]
    attn_weights, mlp_weights, turned_attn, turned_mlp, sem = refs[17:]
    c = lax.axis_index("shard") % 2
    for k in range(8):
        pltpu.make_async_copy(news[k], outs[k], sem.at[k]).start()
    turned_mlp[1, pl.ds(1280, 8), :] = jnp.zeros((8, 128), F32)

    def unpack(xc, carry):
        for src in range(4):
            j = xc * 4 + src
            chunk = back[src, xc].astype(F32)
            turned_attn[0, pl.ds(pl.multiple_of(j * 16, 16), 16), :] = chunk[0:16]
            turned_attn[1, pl.ds(pl.multiple_of(j * 16, 16), 16), :] = chunk[16:32]
            turned_mlp[0, pl.ds(pl.multiple_of(j * 40, 8), 40), :] = chunk[32:72]
            tail = chunk[72:96]
            turn = pltpu.roll(tail, 64, 1)
            straight = lax.broadcast(c, (24, 128)) == 0
            turned_mlp[1, pl.ds(pl.multiple_of(j * 40, 8), 24), :] = jnp.where(straight, tail, turn)
            turned_mlp[1, pl.ds(pl.multiple_of(j * 40 + 24, 8), 16), :] = jnp.where(straight, turn, tail)[:16]
        return carry

    lax.fori_loop(0, 8, unpack, 0)
    for b in range(4):
        cols = slice(b * 128, (b + 1) * 128)
        for pair in range(2):
            block = turned_attn[pair, cols, :].T.astype(BF16)
            for half in range(2):
                attn_weights[2 * pair + (half + c) % 2, :, cols] = block[64 * half : 64 * half + 64]
    for b in range(10):
        cols = slice(b * 128, (b + 1) * 128)
        block = turned_mlp[0, cols, :].T.astype(BF16)
        for half in range(2):
            mlp_weights[(half + c) % 2, :, cols] = block[64 * half : 64 * half + 64]
        mlp_weights[2, :, cols] = turned_mlp[1, cols, :].T[:64].astype(BF16)
    for k in range(8):
        pltpu.make_async_copy(news[k], outs[k], sem.at[k]).wait()


def run_finish(news, back):
    any_spec = pl.BlockSpec(memory_space=pl.ANY)
    vmem = pl.BlockSpec(memory_space=pltpu.VMEM)
    return pl.pallas_call(
        finish_kernel,
        name="finish",
        out_shape=(
            *[jax.ShapeDtypeStruct(v.shape, F32) for v in news],
            jax.ShapeDtypeStruct((4, 64, 512), BF16),
            jax.ShapeDtypeStruct((3, 64, 1280), BF16),
        ),
        in_specs=[any_spec] * 8 + [vmem],
        out_specs=[pl.BlockSpec(memory_space=pltpu.HBM)] * 8 + [vmem] * 2,
        scratch_shapes=[
            pltpu.VMEM((2, 512, 128), F32),
            pltpu.VMEM((2, 1288, 128), F32),
            pltpu.SemaphoreType.DMA((8,)),
        ],
        compiler_params=pltpu.CompilerParams(vmem_limit_bytes=24 << 20),
    )(*news, back)


def rows_first(flat, rows):
    return flat.reshape(flat.shape[0], rows, 16, 128).transpose(1, 2, 0, 3)


def members_first(value):
    rows, _, members, _ = value.shape
    return value.transpose(2, 0, 1, 3).reshape(members, rows * D)


def per_device(attn_grads, mlp_grads, *states):
    states = [rows_first(v, 16) for v in states[:4]] + [rows_first(v, 40) for v in states[4:]]
    args = [attn_grads.transpose(0, 2, 1), mlp_grads.transpose(0, 2, 1), *states]
    *news, back = run_exchange([pltpu.with_memory_space_constraint(v, pltpu.HBM) for v in args])
    *outs, attn_weights, mlp_weights = run_finish(news, back)
    outs = [members_first(v) for v in outs]
    return (*outs, attn_weights.transpose(0, 2, 1), mlp_weights.transpose(0, 2, 1))


def solution(mesh):
    whole = P(None, "tensor", "shard")
    flat = P(None, ("shard", "tensor"))
    return jax.shard_map(
        per_device,
        mesh=mesh,
        in_specs=(whole,) * 2 + (flat,) * 8,
        out_specs=(flat,) * 8 + (whole,) * 2,
        check_vma=False,
    )
```

time: 91.6 us -> 54.7 us (0.60); the launches traced: 90.1 us -> 54.6 us
  local copies, waits for them, and re-layouts: 14.9 us -> 0 us
  other arithmetic: 11.8 us -> 0 us
  Pallas kernels: 62.6 us -> 53.9 us
    unnamed x32 -> x0, local copies, waits for them, and re-layouts: 13.4 us -> none
    pallas_call x1 -> x2, Pallas kernels: 62.6 us -> 53.9 us  [the longest x1 50.4 us: run_exchange(): pl.pallas_call(exchange_kernel, name='exchange', out_shape=(*[jax.ShapeDt...]
    add x2 -> x0, other arithmetic: 7.46 us -> none  [per_device(): average_keep * average + (1.0 - average_keep) * master_new]
    another operation x2 -> x0, other arithmetic: 2.19 us -> none  [the longest x1 1.95 us: per_device(): jnp.stack([even[:, 0:16].reshape(512, 64), odd[:, 0:16].reshape(512, 64),...]
    mul x2 -> x0, other arithmetic: 1.83 us -> none  [advance(): clipped = clip * grads]
    slice x5 -> x0, local copies, waits for them, and re-layouts: 1.36 us -> none  [the longest x1 0.77 us: per_device(): odd[:, 72:88]]
where the time goes in v2:
time: 54.7 us; the launch traced here: 54.6 us
  Pallas kernels  53.9 us (99%)
  between operations  0.65 us (1%)
    pallas_call x1, Pallas kernels, run_exchange(): pl.pallas_call(exchange_kernel, name='exchange', out_shape=(*[jax.ShapeDt...  50.4 us
    pallas_call x1, Pallas kernels, run_finish(): pl.pallas_call(finish_kernel, name='finish', out_shape=(*[jax.ShapeDtypeS...  3.55 us

profile of v2, /device:TPU:1, one launch (start us, length us, event | category | flops | bytes accessed | tf_op | source)
XLA Modules:
  0.0 54.6 jit_solution(6614319086462423072)
XLA Ops:
  0.6 50.4 %exchange.1 = (f32[16,16,4,128]{3,2,1,0:T(4,128)S(1)}, f32[16,16,4,128]{3,2,1,0:T(4,128)S(1)}, f32[16,16,4,128]{3,2,1,0:T(4,128)S(1)}, f32[16,16,4,128]{3,2,1,0:...) custom-call(f32[4,64,512]{2,1,0:T(8,128)} %bitcast.57, ...), custom_call_target="tpu_custom_call" | custom-call | tf_op jit(solution)/shard_map/exchange/pallas_call | solution.py:429
  51.0 3.5 %finish.1 = (f32[16,16,4,128]{3,2,1,0:T(4,128)}, f32[16,16,4,128]{3,2,1,0:T(4,128)}, f32[16,16,4,128]{3,2,1,0:T(4,128)}, f32[16,16,4,128]{3,2,1,0:T(4,128)}, f32...) custom-call(f32[16,16,4,128]{3,2,1,0:T(4,128)S(1)} %get-tuple-elemen, ...), custom_call_target="tpu_custom_call" | custom-call | tf_op jit(solution)/shard_map/finish/pallas_call | solution.py:514

commit v3 on v2

--- a/solution.py
+++ b/solution.py
@@ -59,95 +59,13 @@
     pltpu.make_async_copy(ref, ref, sem).wait()
 
 
-OTHERS = [(dx, dc) for dx in range(4) for dc in range(2)][1:]
-TURNS = (1, 3, 2, 0)
-RING = (0, 1, 3, 2)
-
-
-class Exchange:
-    def __init__(self, forward, held, landed, a_recv, b_recv, c_recv, a_sent, b_sent, c_sent):
-        self.held, self.landed = held, landed
-        self.a_recv, self.b_recv, self.c_recv = a_recv, b_recv, c_recv
-        self.a_sent, self.b_sent, self.c_sent = a_sent, b_sent, c_sent
-        self.z, self.x, self.c, self.y = position()
-        self.forward = forward
-        self.a, self.b = (self.y, self.z) if forward else (self.z, self.y)
-        self.mine = self.x * 2 + self.c
-
-    def at(self, a, x, c, b):
-        return device(b, x, c, a) if self.forward else device(a, x, c, b)
-
-    def target(self, turn, dc):
-        dx = TURNS[turn] if self.forward else (4 - TURNS[turn]) % 4
-        return (self.x + dx) % 4, (self.c + dc) % 2
-
-    def source(self, turn, dc):
-        dx = TURNS[turn] if self.forward else (4 - TURNS[turn]) % 4
-        return (self.x + 4 - dx) % 4, (self.c + dc) % 2
-
-    def send_a(self, da, xc):
-        pltpu.make_async_remote_copy(
-            src_ref=self.held.at[3 + da, xc],
-            dst_ref=self.held.at[da, xc],
-            send_sem=self.a_sent,
-            recv_sem=self.a_recv.at[da, xc],
-            device_id=self.at((self.a + da) % 4, self.x, self.c, self.b),
-            device_id_type=MESH,
-        ).start()
-
-    def origin(self, da):
-        origin = (self.a + 4 - da) % 4
-        return origin, jnp.where(origin == self.b, origin, 4 + origin)
-
-    def pass_b(self, turn):
-        for dc in range(2):
-            x, c = self.target(turn, dc)
-            xc = x * 2 + c
-            for da in RING:
-                origin, slot = self.origin(da)
-                if da:
-                    wait_for(self.held.at[da, xc], self.a_recv.at[da, xc])
-                if TURNS[turn] or dc:
-                    pltpu.make_async_remote_copy(
-                        src_ref=self.held.at[da, xc],
-                        dst_ref=self.landed.at[slot, self.mine],
-                        send_sem=self.b_sent.at[da],
-                        recv_sem=self.b_recv.at[origin, self.mine],
-                        device_id=self.at(self.a, x, c, self.b),
-                        device_id_type=MESH,
-                    ).start()
-                else:
-                    pltpu.make_async_copy(
-                        self.held.at[da, xc], self.landed.at[slot, xc], self.b_recv.at[origin, xc]
-                    ).start()
-
-    def pass_c(self, turn):
-        for dc in range(2):
-            x, c = self.source(turn, dc)
-            xc = x * 2 + c
-            for da in RING:
-                origin, slot = self.origin(da)
-                wait_for(self.landed.at[slot, xc], self.b_recv.at[origin, xc])
-
-                @pl.when(origin != self.b)
-                def _():
-                    pltpu.make_async_remote_copy(
-                        src_ref=self.landed.at[slot, xc],
-                        dst_ref=self.landed.at[self.b, xc],
-                        send_sem=self.c_sent,
-                        recv_sem=self.c_recv.at[self.b, xc],
-                        device_id=self.at(self.a, self.x, self.c, origin),
-                        device_id_type=MESH,
-                    ).start()
-
-    def take_c(self, source, xc):
-        wait_for(self.landed.at[source, xc], self.c_recv.at[source, xc])
-
-    def drain(self):
-        wait_for(self.held.at[pl.ds(4, 3)], self.a_sent)
-        for da in range(4):
-            wait_for(self.held.at[da, pl.ds(0, 7)], self.b_sent.at[da])
-        wait_for(self.held.at[pl.ds(4, 3)], self.c_sent)
+PLANE = [(dx, dc, dy) for dy in range(4) for dx in range(4) for dc in range(2)][1:]
+
+
+def send(src, dst, sent, received, target):
+    pltpu.make_async_remote_copy(
+        src_ref=src, dst_ref=dst, send_sem=sent, recv_sem=received, device_id=target, device_id_type=MESH
+    ).start()
 
 
 def exchange_kernel(
@@ -185,26 +103,18 @@
     flat_sem,
     sum_recv,
     sum_sent,
-    fa_recv,
-    fb_recv,
-    fc_recv,
-    fa_sent,
-    fb_sent,
-    fc_sent,
-    ra_recv,
-    rb_recv,
-    rc_recv,
-    ra_sent,
-    rb_sent,
-    rc_sent,
+    plane_recv,
+    ring_recv,
+    plane_sent,
+    ring_sent,
+    back_ring_recv,
+    back_plane_recv,
+    back_ring_sent,
+    back_plane_sent,
 ):
     z, x, c, y = position()
+    mine = x * 2 + c
     barrier = pltpu.get_barrier_semaphore()
-    for d in range(1, 4):
-        pl.semaphore_signal(barrier, inc=1, device_id=device(z, x, c, (y + d) % 4), device_id_type=MESH)
-        pl.semaphore_signal(barrier, inc=1, device_id=device((z + d) % 4, x, c, y), device_id_type=MESH)
-    for dx, dc in OTHERS:
-        pl.semaphore_signal(barrier, inc=1, device_id=device(z, (x + dx) % 4, (c + dc) % 2, y), device_id_type=MESH)
 
     for pair in range(2):
         for i in range(2):
@@ -214,22 +124,12 @@
         half = pl.ds(pl.multiple_of(64 * ((i + c) % 2), 64), 64)
         pltpu.make_async_copy(mlp_grads.at[i], stack_mlp.at[0, half, :], grad_sem.at[1]).start()
         pltpu.make_async_copy(mlp_grads.at[2], stack_mlp.at[1, pl.ds(64 * i, 64), :], grad_sem.at[1]).start()
-    olds = (
-        (attn_master, mlp_master),
-        (attn_first, mlp_first),
-        (attn_second, mlp_second),
-        (attn_average, mlp_average),
-    )
-    for k, (attn, mlp) in enumerate(olds):
-
-        def fetch(cb, carry, k=k, attn=attn, mlp=mlp):
-            for m in range(4):
-                pltpu.make_async_copy(attn.at[:, cb, m, :], state_attn.at[k, cb, m], state_sem.at[0]).start()
-            for m in range(3):
-                pltpu.make_async_copy(mlp.at[:, cb, m, :], state_mlp.at[k, cb, m], state_sem.at[1]).start()
-            return carry
-
-        lax.fori_loop(0, 16, fetch, 0)
+    for dx, dc, dy in PLANE:
+        pl.semaphore_signal(
+            barrier, inc=1, device_id=device(z, (x + dx) % 4, (c + dc) % 2, (y + dy) % 4), device_id_type=MESH
+        )
+    for dz in range(1, 4):
+        pl.semaphore_signal(barrier, inc=1, device_id=device((z + dz) % 4, x, c, y), device_id_type=MESH)
     turned_mlp[1, pl.ds(1280, 8), :] = jnp.zeros((8, 128), F32)
 
     wait_for(stack_attn, grad_sem.at[0])
@@ -249,7 +149,7 @@
         turned_mlp[1, b * 128 : (b + 1) * 128, :] = block.T
         block = block[:64]
         total = total + jnp.sum((block * block).reshape(8, 8, 128), axis=0)
-    sums[0] = total
+    sums[0] = jnp.sum(total, axis=0, keepdims=True)
 
     straight = (low_lanes(24).astype(jnp.int32) + c) == 1
 
@@ -269,73 +169,92 @@
                 ],
                 axis=0,
             ).astype(BF16)
-            da = (dest + 4 - y) % 4
-            held[jnp.where(da == 0, 0, 3 + da), xc] = packed
+            held[dest, xc] = packed
         return carry
 
     lax.fori_loop(0, 8, pack, 0)
 
-    pl.semaphore_wait(barrier, 13)
-
-    def send_sum(src, slot, dev):
-        pltpu.make_async_remote_copy(
-            src_ref=sums.at[src],
-            dst_ref=sums.at[slot],
-            send_sem=sum_sent.at[slot],
-            recv_sem=sum_recv.at[slot],
-            device_id=dev,
-            device_id_type=MESH,
-        ).start()
-
-    for d in range(1, 4):
-        send_sum(0, 2 + d, device(z, x, c, (y + d) % 4))
-
-    go = Exchange(True, held, landed, fa_recv, fb_recv, fc_recv, fa_sent, fb_sent, fc_sent)
-    for turn in range(4):
-        for dc in range(2):
-            tx, tc = go.target(turn, dc)
-            for da in RING[1:]:
-                go.send_a(da, tx * 2 + tc)
-    go.pass_b(0)
-
-    for slot in range(3, 6):
-        wait_for(sums.at[slot], sum_recv.at[slot])
-    sums[1] = sums[0] + sums[3] + sums[4] + sums[5]
-    for k, (dx, dc) in enumerate(OTHERS):
-        send_sum(1, 6 + k, device(z, (x + dx) % 4, (c + dc) % 2, y))
-
-    go.pass_b(1)
-    go.pass_c(0)
-
-    for slot in range(6, 13):
-        wait_for(sums.at[slot], sum_recv.at[slot])
+    pl.semaphore_wait(barrier, len(PLANE) + 3)
+
+    for k, (dx, dc, dy) in enumerate(PLANE):
+        to = device(z, (x + dx) % 4, (c + dc) % 2, (y + dy) % 4)
+        send(sums.at[0], sums.at[2 + k], sum_sent.at[0], sum_recv.at[2 + k], to)
+
+    def plane_slot(origin):
+        return jnp.where(origin == z, origin, 4 + origin)
+
+    for step in range(4):
+        for dy in range(4):
+            dx, to_y = (step + dy) % 4, (y + dy) % 4
+            for dc in range(2):
+                to_x, to_c = (x + dx) % 4, (c + dc) % 2
+                src = held.at[to_y, to_x * 2 + to_c]
+                dst = landed.at[plane_slot(y), mine]
+                if dx or dy or dc:
+                    send(src, dst, plane_sent.at[min(dy, 1)], plane_recv.at[y, mine], device(z, to_x, to_c, to_y))
+                else:
+                    pltpu.make_async_copy(src, dst, plane_recv.at[y, mine]).start()
+
+    olds = (
+        (attn_master, mlp_master),
+        (attn_first, mlp_first),
+        (attn_second, mlp_second),
+        (attn_average, mlp_average),
+    )
+    for k, (attn, mlp) in enumerate(olds):
+
+        def fetch(cb, carry, k=k, attn=attn, mlp=mlp):
+            for m in range(4):
+                pltpu.make_async_copy(attn.at[:, cb, m, :], state_attn.at[k, cb, m], state_sem.at[0]).start()
+            for m in range(3):
+                pltpu.make_async_copy(mlp.at[:, cb, m, :], state_mlp.at[k, cb, m], state_sem.at[1]).start()
+            return carry
+
+        lax.fori_loop(0, 16, fetch, 0)
+
+    def ring(step):
+        for dy in range(4):
+            dx, from_y = (step + dy) % 4, (y + 4 - dy) % 4
+            slot = plane_slot(from_y)
+            for dc in range(2):
+                xc = (x + 4 - dx) % 4 * 2 + (c + dc) % 2
+                wait_for(landed.at[slot, xc], plane_recv.at[from_y, xc])
+
+                @pl.when(from_y != z)
+                def _():
+                    send(landed.at[slot, xc], landed.at[z, xc], ring_sent, ring_recv.at[z, xc], device(from_y, x, c, y))
+
+    ring(0)
+    value = sums[0]
+    for k in range(len(PLANE)):
+        wait_for(sums.at[2 + k], sum_recv.at[2 + k])
+        value = value + sums[2 + k]
+    sums[1] = value
+    ring(1)
+    ahead = 2 + len(PLANE)
+    for dz in range(1, 4):
+        send(sums.at[1], sums.at[ahead + dz - 1], sum_sent.at[1], sum_recv.at[ahead + dz - 1], device((z + dz) % 4, x, c, y))
+    ring(2)
+    ring(3)
     value = sums[1]
-    for slot in range(6, 13):
-        value = value + sums[slot]
-    sums[2] = value
-    for d in range(1, 4):
-        send_sum(2, 12 + d, device((z + d) % 4, x, c, y))
-
-    go.pass_b(2)
-    go.pass_c(1)
-    go.pass_b(3)
-    go.pass_c(2)
-
-    for slot in range(13, 16):
-        wait_for(sums.at[slot], sum_recv.at[slot])
-    grand = jnp.sum(sums[2] + sums[13] + sums[14] + sums[15], keepdims=True)
+    for dz in range(3):
+        wait_for(sums.at[ahead + dz], sum_recv.at[ahead + dz])
+        value = value + sums[ahead + dz]
+    grand = jnp.sum(value, keepdims=True)
     clip = jnp.minimum(1.0, clip_level / jnp.sqrt(grand / COUNT + 1e-06))
 
     wait_for(state_attn, state_sem.at[0])
     wait_for(state_mlp, state_sem.at[1])
 
-    ret = Exchange(False, held_back, back, ra_recv, rb_recv, rc_recv, ra_sent, rb_sent, rc_sent)
     low = low_lanes(ROWS)
 
-    def work(turn):
-        xs, _ = go.source(turn, 0)
-
-        def one(source, place, da):
+    def column(step, from_z):
+        return (x + 8 - (step + y + 4 - from_z) % 4) % 4
+
+    def work(step):
+        xs = (x + 4 - (step + y + 4 - z) % 4) % 4
+
+        def one(source, place):
             cb = source * 4 + xs
             even, odd = split_halves(landed[source, xs * 2].astype(F32), landed[source, xs * 2 + 1].astype(F32))
             pieces = (
@@ -360,18 +279,51 @@
             held_back[place, xs * 2] = jnp.where(low, first_half, other).astype(BF16)
             held_back[place, xs * 2 + 1] = jnp.where(low, other, first_half).astype(BF16)
 
-        one(z, 0, 0)
-
-        def distant(da, carry):
-            source = (z + da) % 4
+        def pass_on(dz):
             for dc in range(2):
-                go.take_c(source, xs * 2 + dc)
-            one(source, 3 + da, da)
+                xc = xs * 2 + dc
+                send(
+                    held_back.at[3 + dz, xc],
+                    held_back.at[dz, xc],
+                    back_ring_sent,
+                    back_ring_recv.at[dz, xc],
+                    device((z + dz) % 4, x, c, y),
+                )
+
+        def distant(dz, carry):
+            source = (z + dz) % 4
             for dc in range(2):
-                ret.send_a(da, xs * 2 + dc)
+                wait_for(landed.at[source, xs * 2 + dc], ring_recv.at[source, xs * 2 + dc])
+            one(source, 3 + dz)
+
+            @pl.when(dz > 1)
+            def _():
+                pass_on(dz - 1)
+
             return carry
 
         lax.fori_loop(1, 4, distant, 0)
+        one(z, 0)
+        pass_on(3)
+
+    def spread(step):
+        for dz in range(4):
+            from_z = (z + 4 - dz) % 4
+            xs = column(step, from_z)
+            for dc in range(2):
+                xc = xs * 2 + dc
+                src, dst, received = held_back.at[dz, xc], back.at[y, mine], back_plane_recv.at[y, mine]
+                if dz:
+                    wait_for(src, back_ring_recv.at[dz, xc])
+                here = jnp.logical_and(xc == mine, from_z == y)
+
+                @pl.when(here)
+                def _():
+                    pltpu.make_async_copy(src, dst, received).start()
+
+                @pl.when(jnp.logical_not(here))
+                def _():
+                    send(src, dst, back_plane_sent.at[jnp.where(from_z == y, 0, 1)], received, device(z, xs, dc, from_z))
 
     news = (
         (attn_master_new, mlp_master_new),
@@ -380,8 +332,8 @@
         (attn_average_new, mlp_average_new),
     )
 
-    def store(turn):
-        xs, _ = go.source(turn, 0)
+    def store(step):
+        xs = (x + 4 - (step + y + 4 - z) % 4) % 4
 
         def one(zs, carry):
             cb = zs * 4 + xs
@@ -396,29 +348,27 @@
 
     work(0)
     work(1)
-    ret.pass_b(0)
-    go.pass_c(3)
+    spread(0)
     work(2)
-    ret.pass_b(1)
-    ret.pass_c(0)
+    spread(1)
     work(3)
-    ret.pass_b(2)
-    ret.pass_c(1)
-    ret.pass_b(3)
+    spread(2)
     store(0)
-    ret.pass_c(2)
+    spread(3)
     store(1)
-    ret.pass_c(3)
     store(2)
     store(3)
-    for d in range(1, 4):
+    for src in range(4):
         for xc in range(8):
-            ret.take_c((y + d) % 4, xc)
-
-    go.drain()
-    ret.drain()
-    for slot in range(3, 16):
-        wait_for(sums.at[slot], sum_sent.at[slot])
+            wait_for(back.at[src, xc], back_plane_recv.at[src, xc])
+
+    wait_for(sums.at[pl.ds(2, len(PLANE))], sum_sent.at[0])
+    wait_for(sums.at[pl.ds(2, 3)], sum_sent.at[1])
+    wait_for(landed.at[pl.ds(0, 3)], ring_sent)
+    wait_for(landed.at[pl.ds(0, 3)], back_ring_sent)
+    for sem in (plane_sent, back_plane_sent):
+        wait_for(landed.at[0, pl.ds(0, 7)], sem.at[0])
+        wait_for(landed.at[pl.ds(0, 3)], sem.at[1])
     wait_for(state_attn, flat_sem.at[0])
     wait_for(state_mlp, flat_sem.at[1])
 
@@ -432,7 +382,7 @@
         out_shape=(
             *[jax.ShapeDtypeStruct((16, 16, 4, 128), F32)] * 4,
             *[jax.ShapeDtypeStruct((40, 16, 3, 128), F32)] * 4,
-            jax.ShapeDtypeStruct((8, 8, ROWS, 128), BF16),
+            jax.ShapeDtypeStruct((4, 8, ROWS, 128), BF16),
         ),
         in_specs=[pl.BlockSpec(memory_space=pltpu.HBM)] * 10,
         out_specs=[any_spec] * 9,
@@ -441,29 +391,25 @@
             pltpu.VMEM((2, 128, 1280), F32),
             pltpu.VMEM((2, 512, 128), F32),
             pltpu.VMEM((2, 1288, 128), F32),
-            pltpu.VMEM((7, 8, ROWS, 128), BF16),
+            pltpu.VMEM((4, 8, ROWS, 128), BF16),
             pltpu.VMEM((8, 8, ROWS, 128), BF16),
             pltpu.VMEM((7, 8, ROWS, 128), BF16),
             pltpu.VMEM((4, 16, 4, 16, 128), F32),
             pltpu.VMEM((4, 16, 3, 40, 128), F32),
-            pltpu.VMEM((16, 8, 128), F32),
+            pltpu.VMEM((36, 1, 128), F32),
             dma((2,)),
             dma((2,)),
             dma((2,)),
-            dma((16,)),
-            dma((16,)),
+            dma((36,)),
+            dma((2,)),
             dma((4, 8)),
+            dma((4, 8)),
+            dma((2,)),
+            dma,
             dma((4, 8)),
             dma((4, 8)),
             dma,
-            dma((4,)),
-            dma,
-            dma((4, 8)),
-            dma((4, 8)),
-            dma((4, 8)),
-            dma,
-            dma((4,)),
-            dma,
+            dma((2,)),
         ],
         compiler_params=pltpu.CompilerParams(collective_id=0, has_side_effects=True, vmem_limit_bytes=32 << 20),
     )(*args)

time: 54.7 us -> 47.3 us (0.86)
  Pallas kernels: 53.9 us -> 46.5 us
    pallas_call x1, Pallas kernels: 50.4 us -> 42.9 us  [run_exchange(): pl.pallas_call(exchange_kernel, name='exchange', out_shape=(*[jax.ShapeDt...]
where the time goes in v3:
time: 47.3 us; the launch traced here: 47.1 us
  Pallas kernels  46.5 us (98%)
  between operations  0.65 us (1%)
    pallas_call x1, Pallas kernels, run_exchange(): pl.pallas_call(exchange_kernel, name='exchange', out_shape=(*[jax.ShapeDt...  42.9 us
    pallas_call x1, Pallas kernels, run_finish(): pl.pallas_call(finish_kernel, name='finish', out_shape=(*[jax.ShapeDtypeS...  3.55 us

profile of v3, /device:TPU:1, one launch (start us, length us, event | category | flops | bytes accessed | tf_op | source)
XLA Modules:
  0.0 47.1 jit_solution(11979038654941586915)
XLA Ops:
  0.6 42.9 %exchange.1 = (f32[16,16,4,128]{3,2,1,0:T(4,128)S(1)}, f32[16,16,4,128]{3,2,1,0:T(4,128)S(1)}, f32[16,16,4,128]{3,2,1,0:T(4,128)S(1)}, f32[16,16,4,128]{3,2,1,0:...) custom-call(f32[4,64,512]{2,1,0:T(8,128)} %bitcast.57, ...), custom_call_target="tpu_custom_call" | custom-call | tf_op jit(solution)/shard_map/exchange/pallas_call | solution.py:379
  43.6 3.5 %finish.1 = (f32[16,16,4,128]{3,2,1,0:T(4,128)}, f32[16,16,4,128]{3,2,1,0:T(4,128)}, f32[16,16,4,128]{3,2,1,0:T(4,128)}, f32[16,16,4,128]{3,2,1,0:T(4,128)}, f32...) custom-call(f32[16,16,4,128]{3,2,1,0:T(4,128)S(1)} %get-tuple-elemen, ...), custom_call_target="tpu_custom_call" | custom-call | tf_op jit(solution)/shard_map/finish/pallas_call | solution.py:460

commit v4 on v3

--- a/solution.py
+++ b/solution.py
@@ -59,7 +59,7 @@
     pltpu.make_async_copy(ref, ref, sem).wait()
 
 
-PLANE = [(dx, dc, dy) for dy in range(4) for dx in range(4) for dc in range(2)][1:]
+PLANE = [(dx, dc, dz) for dz in range(4) for dx in range(4) for dc in range(2)][1:]
 
 
 def send(src, dst, sent, received, target):
@@ -95,6 +95,7 @@
     held,
     landed,
     held_back,
+    relay,
     state_attn,
     state_mlp,
     sums,
@@ -103,10 +104,8 @@
     flat_sem,
     sum_recv,
     sum_sent,
-    plane_recv,
-    ring_recv,
-    plane_sent,
-    ring_sent,
+    grad_recv,
+    grad_sent,
     back_ring_recv,
     back_plane_recv,
     back_ring_sent,
@@ -124,12 +123,25 @@
         half = pl.ds(pl.multiple_of(64 * ((i + c) % 2), 64), 64)
         pltpu.make_async_copy(mlp_grads.at[i], stack_mlp.at[0, half, :], grad_sem.at[1]).start()
         pltpu.make_async_copy(mlp_grads.at[2], stack_mlp.at[1, pl.ds(64 * i, 64), :], grad_sem.at[1]).start()
-    for dx, dc, dy in PLANE:
-        pl.semaphore_signal(
-            barrier, inc=1, device_id=device(z, (x + dx) % 4, (c + dc) % 2, (y + dy) % 4), device_id_type=MESH
-        )
-    for dz in range(1, 4):
-        pl.semaphore_signal(barrier, inc=1, device_id=device((z + dz) % 4, x, c, y), device_id_type=MESH)
+    def announce(to):
+        pl.semaphore_signal(barrier, inc=1, device_id=to, device_id_type=MESH)
+
+    for dz in range(4):
+        for dx in range(4):
+            for dc in range(2):
+                to = device((z + dz) % 4, (x + dx) % 4, (c + dc) % 2, z)
+                if dz or dx or dc:
+                    announce(to)
+                else:
+
+                    @pl.when(y != z)
+                    def _():
+                        announce(to)
+
+    for dx, dc, dz in PLANE:
+        announce(device((z + dz) % 4, (x + dx) % 4, (c + dc) % 2, y))
+    for dy in range(1, 4):
+        announce(device(z, x, c, (y + dy) % 4))
     turned_mlp[1, pl.ds(1280, 8), :] = jnp.zeros((8, 128), F32)
 
     wait_for(stack_attn, grad_sem.at[0])
@@ -174,26 +186,32 @@
 
     lax.fori_loop(0, 8, pack, 0)
 
-    pl.semaphore_wait(barrier, len(PLANE) + 3)
-
-    for k, (dx, dc, dy) in enumerate(PLANE):
-        to = device(z, (x + dx) % 4, (c + dc) % 2, (y + dy) % 4)
+    pl.semaphore_wait(barrier, jnp.where(y == z, 31, 32) + len(PLANE) + 3)
+
+    for k, (dx, dc, dz) in enumerate(PLANE):
+        to = device((z + dz) % 4, (x + dx) % 4, (c + dc) % 2, y)
         send(sums.at[0], sums.at[2 + k], sum_sent.at[0], sum_recv.at[2 + k], to)
 
-    def plane_slot(origin):
-        return jnp.where(origin == z, origin, 4 + origin)
-
+    alone = [None] * 4
     for step in range(4):
-        for dy in range(4):
-            dx, to_y = (step + dy) % 4, (y + dy) % 4
+        for m in range(4):
+            dx, to_y = (step + m) % 4, (y + m + 4 - z) % 4
             for dc in range(2):
                 to_x, to_c = (x + dx) % 4, (c + dc) % 2
-                src = held.at[to_y, to_x * 2 + to_c]
-                dst = landed.at[plane_slot(y), mine]
-                if dx or dy or dc:
-                    send(src, dst, plane_sent.at[min(dy, 1)], plane_recv.at[y, mine], device(z, to_x, to_c, to_y))
+                src, dst, received = held.at[to_y, to_x * 2 + to_c], landed.at[z, mine], grad_recv.at[z, mine]
+                to = device(y, to_x, to_c, to_y)
+                if dx or dc:
+                    send(src, dst, grad_sent.at[4], received, to)
                 else:
-                    pltpu.make_async_copy(src, dst, plane_recv.at[y, mine]).start()
+                    alone[m] = jnp.logical_and(y == z, to_y == y)
+
+                    @pl.when(alone[m])
+                    def _():
+                        pltpu.make_async_copy(src, dst, received).start()
+
+                    @pl.when(jnp.logical_not(alone[m]))
+                    def _():
+                        send(src, dst, grad_sent.at[m], received, to)
 
     olds = (
         (attn_master, mlp_master),
@@ -201,9 +219,11 @@
         (attn_second, mlp_second),
         (attn_average, mlp_average),
     )
-    for k, (attn, mlp) in enumerate(olds):
-
-        def fetch(cb, carry, k=k, attn=attn, mlp=mlp):
+
+    def load(k):
+        attn, mlp = olds[k]
+
+        def fetch(cb, carry):
             for m in range(4):
                 pltpu.make_async_copy(attn.at[:, cb, m, :], state_attn.at[k, cb, m], state_sem.at[0]).start()
             for m in range(3):
@@ -212,34 +232,23 @@
 
         lax.fori_loop(0, 16, fetch, 0)
 
-    def ring(step):
-        for dy in range(4):
-            dx, from_y = (step + dy) % 4, (y + 4 - dy) % 4
-            slot = plane_slot(from_y)
-            for dc in range(2):
-                xc = (x + 4 - dx) % 4 * 2 + (c + dc) % 2
-                wait_for(landed.at[slot, xc], plane_recv.at[from_y, xc])
-
-                @pl.when(from_y != z)
-                def _():
-                    send(landed.at[slot, xc], landed.at[z, xc], ring_sent, ring_recv.at[z, xc], device(from_y, x, c, y))
-
-    ring(0)
+    load(0)
+    load(1)
+    load(2)
     value = sums[0]
     for k in range(len(PLANE)):
         wait_for(sums.at[2 + k], sum_recv.at[2 + k])
         value = value + sums[2 + k]
     sums[1] = value
-    ring(1)
+    load(3)
     ahead = 2 + len(PLANE)
-    for dz in range(1, 4):
-        send(sums.at[1], sums.at[ahead + dz - 1], sum_sent.at[1], sum_recv.at[ahead + dz - 1], device((z + dz) % 4, x, c, y))
-    ring(2)
-    ring(3)
+    for dy in range(1, 4):
+        to = device(z, x, c, (y + dy) % 4)
+        send(sums.at[1], sums.at[ahead + dy - 1], sum_sent.at[1], sum_recv.at[ahead + dy - 1], to)
     value = sums[1]
-    for dz in range(3):
-        wait_for(sums.at[ahead + dz], sum_recv.at[ahead + dz])
-        value = value + sums[ahead + dz]
+    for dy in range(3):
+        wait_for(sums.at[ahead + dy], sum_recv.at[ahead + dy])
+        value = value + sums[ahead + dy]
     grand = jnp.sum(value, keepdims=True)
     clip = jnp.minimum(1.0, clip_level / jnp.sqrt(grand / COUNT + 1e-06))
 
@@ -248,13 +257,14 @@
 
     low = low_lanes(ROWS)
 
-    def column(step, from_z):
-        return (x + 8 - (step + y + 4 - from_z) % 4) % 4
+    def column(step, dz):
+        return (x + 4 - (step + y + dz) % 4) % 4
 
     def work(step):
-        xs = (x + 4 - (step + y + 4 - z) % 4) % 4
-
-        def one(source, place):
+        def one(dz):
+            source, xs = (z + dz) % 4, column(step, dz)
+            for dc in range(2):
+                wait_for(landed.at[source, xs * 2 + dc], grad_recv.at[source, xs * 2 + dc])
             cb = source * 4 + xs
             even, odd = split_halves(landed[source, xs * 2].astype(F32), landed[source, xs * 2 + 1].astype(F32))
             pieces = (
@@ -276,54 +286,66 @@
                 new.append(values[0])
             first_half = jnp.concatenate(new[:4], axis=0)
             other = pltpu.roll(jnp.concatenate(new[4:] + [jnp.zeros((8, 128), F32)], axis=0), 64, 1)
-            held_back[place, xs * 2] = jnp.where(low, first_half, other).astype(BF16)
-            held_back[place, xs * 2 + 1] = jnp.where(low, other, first_half).astype(BF16)
-
-        def pass_on(dz):
+            held_back[dz, xs * 2] = jnp.where(low, first_half, other).astype(BF16)
+            held_back[dz, xs * 2 + 1] = jnp.where(low, other, first_half).astype(BF16)
+
+        def give(dz, may_stay):
+            xs = column(step, dz)
             for dc in range(2):
-                xc = xs * 2 + dc
-                send(
-                    held_back.at[3 + dz, xc],
-                    held_back.at[dz, xc],
-                    back_ring_sent,
-                    back_ring_recv.at[dz, xc],
-                    device((z + dz) % 4, x, c, y),
-                )
+                src, received = held_back.at[dz, xs * 2 + dc], back_plane_recv.at[z, mine]
+                stays = jnp.logical_and(xs == x, c == dc) if may_stay else False
+
+                def start(dst):
+                    if may_stay:
+
+                        @pl.when(stays)
+                        def _():
+                            pltpu.make_async_copy(src, dst, received).start()
+
+                        @pl.when(jnp.logical_not(stays))
+                        def _():
+                            send(src, dst, back_plane_sent.at[0], received, device(z, xs, dc, y))
+
+                    else:
+                        send(src, dst, back_plane_sent.at[1], received, device((z + dz) % 4, xs, dc, y))
+
+                @pl.when(y == z)
+                def _():
+                    start(back.at[y, mine])
+
+                @pl.when(y != z)
+                def _():
+                    start(relay.at[z, mine])
 
         def distant(dz, carry):
-            source = (z + dz) % 4
-            for dc in range(2):
-                wait_for(landed.at[source, xs * 2 + dc], ring_recv.at[source, xs * 2 + dc])
-            one(source, 3 + dz)
+            one(dz)
 
             @pl.when(dz > 1)
             def _():
-                pass_on(dz - 1)
+                give(dz - 1, False)
 
             return carry
 
         lax.fori_loop(1, 4, distant, 0)
-        one(z, 0)
-        pass_on(3)
+        one(0)
+        give(3, False)
+        return functools.partial(give, 0, True)
 
     def spread(step):
-        for dz in range(4):
-            from_z = (z + 4 - dz) % 4
-            xs = column(step, from_z)
-            for dc in range(2):
-                xc = xs * 2 + dc
-                src, dst, received = held_back.at[dz, xc], back.at[y, mine], back_plane_recv.at[y, mine]
-                if dz:
-                    wait_for(src, back_ring_recv.at[dz, xc])
-                here = jnp.logical_and(xc == mine, from_z == y)
-
-                @pl.when(here)
-                def _():
-                    pltpu.make_async_copy(src, dst, received).start()
-
-                @pl.when(jnp.logical_not(here))
-                def _():
-                    send(src, dst, back_plane_sent.at[jnp.where(from_z == y, 0, 1)], received, device(z, xs, dc, from_z))
+        def group(k, carry):
+            dz = (k + y) % 4
+            from_z, from_x = (z + 4 - dz) % 4, (x + step + y + dz) % 4
+
+            @pl.when(from_z != y)
+            def _():
+                for dc in range(2):
+                    xc = from_x * 2 + dc
+                    wait_for(relay.at[from_z, xc], back_plane_recv.at[from_z, xc])
+                    send(relay.at[from_z, xc], back.at[y, xc], back_ring_sent, back_ring_recv.at[y, xc], device(z, x, c, from_z))
+
+            return carry
+
+        lax.fori_loop(0, 4, group, 0)
 
     news = (
         (attn_master_new, mlp_master_new),
@@ -333,10 +355,8 @@
     )
 
     def store(step):
-        xs = (x + 4 - (step + y + 4 - z) % 4) % 4
-
-        def one(zs, carry):
-            cb = zs * 4 + xs
+        def one(dz, carry):
+            cb = (z + dz) % 4 * 4 + column(step, dz)
             for k, (attn, mlp) in enumerate(news):
                 for m in range(4):
                     pltpu.make_async_copy(state_attn.at[k, cb, m], attn.at[:, cb, m, :], flat_sem.at[0]).start()
@@ -346,29 +366,33 @@
 
         lax.fori_loop(0, 4, one, 0)
 
-    work(0)
-    work(1)
-    spread(0)
-    work(2)
-    spread(1)
-    work(3)
-    spread(2)
-    store(0)
-    spread(3)
-    store(1)
-    store(2)
-    store(3)
-    for src in range(4):
-        for xc in range(8):
-            wait_for(back.at[src, xc], back_plane_recv.at[src, xc])
+    own = work(0)
+    for step in range(1, 4):
+        following = work(step)
+        own()
+        own = following
+    own()
+    for step in range(4):
+        spread(step)
+        store(step)
+    for xc in range(8):
+        wait_for(back.at[y, xc], back_plane_recv.at[y, xc])
+        for dy in range(1, 4):
+            src = (y + dy) % 4
+            wait_for(back.at[src, xc], back_ring_recv.at[src, xc])
 
     wait_for(sums.at[pl.ds(2, len(PLANE))], sum_sent.at[0])
     wait_for(sums.at[pl.ds(2, 3)], sum_sent.at[1])
-    wait_for(landed.at[pl.ds(0, 3)], ring_sent)
-    wait_for(landed.at[pl.ds(0, 3)], back_ring_sent)
-    for sem in (plane_sent, back_plane_sent):
-        wait_for(landed.at[0, pl.ds(0, 7)], sem.at[0])
-        wait_for(landed.at[pl.ds(0, 3)], sem.at[1])
+    wait_for(held_back.at[:, pl.ds(0, 7)], grad_sent.at[4])
+    for m in range(4):
+
+        @pl.when(jnp.logical_not(alone[m]))
+        def _():
+            wait_for(held.at[0, 0], grad_sent.at[m])
+
+    wait_for(held_back.at[pl.ds(0, 3)], back_ring_sent)
+    wait_for(held_back.at[0, pl.ds(0, 7)], back_plane_sent.at[0])
+    wait_for(held_back.at[pl.ds(0, 3)], back_plane_sent.at[1])
     wait_for(state_attn, flat_sem.at[0])
     wait_for(state_mlp, flat_sem.at[1])
 
@@ -392,8 +416,9 @@
             pltpu.VMEM((2, 512, 128), F32),
             pltpu.VMEM((2, 1288, 128), F32),
             pltpu.VMEM((4, 8, ROWS, 128), BF16),
-            pltpu.VMEM((8, 8, ROWS, 128), BF16),
-            pltpu.VMEM((7, 8, ROWS, 128), BF16),
+            pltpu.VMEM((4, 8, ROWS, 128), BF16),
+            pltpu.VMEM((4, 8, ROWS, 128), BF16),
+            pltpu.VMEM((4, 8, ROWS, 128), BF16),
             pltpu.VMEM((4, 16, 4, 16, 128), F32),
             pltpu.VMEM((4, 16, 3, 40, 128), F32),
             pltpu.VMEM((36, 1, 128), F32),
@@ -403,9 +428,7 @@
             dma((36,)),
             dma((2,)),
             dma((4, 8)),
-            dma((4, 8)),
-            dma((2,)),
-            dma,
+            dma((5,)),
             dma((4, 8)),
             dma((4, 8)),
             dma,

time: 47.3 us -> 44 us (0.930)
  Pallas kernels: 46.5 us -> 43.2 us
    pallas_call x1, Pallas kernels: 42.9 us -> 39.6 us  [run_exchange(): pl.pallas_call(exchange_kernel, name='exchange', out_shape=(*[jax.ShapeDt...]
where the time goes in v4:
time: 44 us; the launch traced here: 43.8 us
  Pallas kernels  43.2 us (98%)
  between operations  0.65 us (1%)
    pallas_call x1, Pallas kernels, run_exchange(): pl.pallas_call(exchange_kernel, name='exchange', out_shape=(*[jax.ShapeDt...  39.6 us
    pallas_call x1, Pallas kernels, run_finish(): pl.pallas_call(finish_kernel, name='finish', out_shape=(*[jax.ShapeDtypeS...  3.55 us

profile of v4, /device:TPU:1, one launch (start us, length us, event | category | flops | bytes accessed | tf_op | source)
XLA Modules:
  0.0 43.8 jit_solution(17720647094420440454)
XLA Ops:
  0.6 39.6 %exchange.1 = (f32[16,16,4,128]{3,2,1,0:T(4,128)S(1)}, f32[16,16,4,128]{3,2,1,0:T(4,128)S(1)}, f32[16,16,4,128]{3,2,1,0:T(4,128)S(1)}, f32[16,16,4,128]{3,2,1,0:...) custom-call(f32[4,64,512]{2,1,0:T(8,128)} %bitcast.57, ...), custom_call_target="tpu_custom_call" | custom-call | tf_op jit(solution)/shard_map/exchange/pallas_call | solution.py:403
  40.3 3.5 %finish.1 = (f32[16,16,4,128]{3,2,1,0:T(4,128)}, f32[16,16,4,128]{3,2,1,0:T(4,128)}, f32[16,16,4,128]{3,2,1,0:T(4,128)}, f32[16,16,4,128]{3,2,1,0:T(4,128)}, f32...) custom-call(f32[16,16,4,128]{3,2,1,0:T(4,128)S(1)} %get-tuple-elemen, ...), custom_call_target="tpu_custom_call" | custom-call | tf_op jit(solution)/shard_map/finish/pallas_call | solution.py:483
